TPU v7x, 256 devices: a whole 4x4x8 slice. The times are simulated.
256 devices in a mesh: lblk: 32 (over z_hi, x, core), tile: 8 (over y, z_lo).
Axes of the slice: x: 4, y: 4, z: 8 (z_hi: 4, z_lo: 2; z = z_hi * 2 + z_lo), core: 2. Of those that a mesh axis runs over, the one named last changes fastest.
Arguments:
- wavefunction: float32 [4096, 2, 64, 128], P('lblk', None, 'tile'), may hold values from -6 to 6
- l_table: int32 [4096, 2], P('lblk'), may hold values from 0 to 15
- coupling: float32 [32, 8, 128, 128], P('lblk'), may hold values from -2 to 2
- selection: int32 [32, 8], P('lblk'), may hold values 0 or 1
- dipole: float32 [32, 2, 128, 128], P('lblk'), may hold values from -0.5 to 0.5
- field: float32 [1], replicated, may hold values from -0.1 to 0.1
Outputs:
- propagated: float32 [4096, 2, 64, 128], P('lblk', None, 'tile')
All inputs are finite; a program needn't handle non-finite values. No bound on the sum of `selection` on one device may be relied on, other than what follows from the above.
Results may differ from a plain program's by a relative error of at most 0.0001.
Values sent between devices are 32-bit elements; how exact they have to be, the bound alone decides.
No kernel may reach another device: no remote copies, remote signals or barrier semaphores. Data moves between devices by JAX's collectives and lax.ppermute only.
A program may use at most 64 MiB of HBM per device.

v0:
```python
import functools

import jax
import jax.numpy as jnp
from jax import lax
from jax.experimental import pallas as pl
from jax.experimental.pallas import tpu as pltpu
from jax.sharding import PartitionSpec as P

NMP = 8
TAYLOR = 4

time_step = 0.03
grid_step = 0.5
radius_start = 8.0

NEAR = -0.5 * 16.0 / (12.0 * grid_step * grid_step)
FAR = 0.5 * 1.0 / (12.0 * grid_step * grid_step)
CENTRE = 2.0 * 0.5 * 30.0 / (12.0 * grid_step * grid_step)

F32 = jnp.float32
BF16 = jnp.bfloat16


def params(limit=40 << 20):
    return pltpu.CompilerParams(dimension_semantics=None, vmem_limit_bytes=limit)


def cost(flops, moved):
    return pl.CostEstimate(flops=flops, bytes_accessed=moved, transcendentals=0)


def whole(shape):
    zeros = (0,) * len(shape)
    return pl.BlockSpec(shape, lambda *_: zeros)


def row_spec():
    return pl.BlockSpec((1, 2, 128, 128), lambda i: (i, 0, 0, 0))


SCALAR = pl.BlockSpec(memory_space=pltpu.SMEM)


def split(value):
    high = value.astype(BF16)
    return high, (value - high.astype(F32)).astype(BF16)


def row_radius(i):
    row = lax.axis_index("tile") * 8 + i
    return radius_start + grid_step * row.astype(F32)


def col_radius(shape):
    col = lax.broadcasted_iota(jnp.int32, shape, len(shape) - 1) % 128
    return radius_start + grid_step * col.astype(F32)


def natural(ref, i, part):
    return ref[pl.ds(part * 8 + i, 128, stride=16), :]


def both(ref, i, first, row):
    if first:
        return jnp.concatenate([natural(ref, i, 0), natural(ref, i, 1)], axis=1)
    return jnp.concatenate([ref[row, 0], ref[row, 1]], axis=1)


def operand(value):
    high, low = split(value)
    return jnp.concatenate([high, low, high], axis=0)


def stacked(matrix):
    high, low = split(matrix)
    return jnp.concatenate([high, high, low], axis=1)


def edges_kernel(psi_ref, h1_ref, h2_ref):
    even = lax.rem(lax.axis_index("tile"), 2) == 0

    def store(ref, start):
        for row in range(2):
            for part in range(2):
                ref[row, part] = natural(psi_ref, start + row, part)

    store(h1_ref, jnp.where(even, 6, 0))
    store(h2_ref, jnp.where(even, 0, 6))


def weights_kernel(sel_ref, coup_ref, l_ref, wcat_ref, radial_ref, ang_ref):
    for k in range(NMP):
        matrix = coup_ref[0, k]
        matrix = 0.5 * (matrix + matrix.T) * sel_ref[0, k].astype(F32)
        wcat_ref[pl.ds(k * 128, 128), :] = stacked(matrix)
    offset = lax.axis_index("tile") * 8
    rows = lax.broadcasted_iota(jnp.int32, (8, 256), 0) + offset
    one = radius_start + grid_step * rows.astype(F32)
    two = col_radius((8, 256))
    larger = jnp.maximum(one, two)
    ratio = jnp.minimum(one, two) / larger
    term = 1.0 / larger
    for k in range(NMP):
        radial_ref[k] = term
        if k < NMP - 1:
            term = term * ratio
    for e in range(2):
        ang = l_ref[:, e : e + 1].astype(F32)
        ang_ref[e] = jnp.broadcast_to(ang * (ang + 1.0) / 2.0, (128, 128))


def dipole_kernel(field_ref, own_ref, below_ref, d1_ref, d2_ref):
    even = lax.rem(lax.axis_index("lblk"), 2) == 0
    strength = field_ref[0]
    for e in range(2):
        up = stacked(own_ref[0, e] * strength)
        down = stacked(below_ref[0, e].T * strength)
        rows = pl.ds(e * 128, 128)

        @pl.when(even)
        def _():
            d1_ref[rows, :] = up
            d2_ref[rows, :] = down

        @pl.when(jnp.logical_not(even))
        def _():
            d1_ref[rows, :] = down
            d2_ref[rows, :] = up


def dipole_part(i, d_ref, other):
    out = jnp.dot(d_ref[...], operand(other), preferred_element_type=F32)
    return row_radius(i) * out[:128] + col_radius((1, 256)) * out[128:]


def local_kernel(first, step, w_ref, other_ref, psi_ref, wcat_ref, d_ref, radial_ref, ang_ref, q_ref):
    i = pl.program_id(0)
    mine = both(w_ref, i, first, i)
    prod = jnp.dot(wcat_ref[...], operand(mine), preferred_element_type=F32)
    total = dipole_part(i, d_ref, both(other_ref, i, first, 0))
    for k in range(NMP):
        total = total + radial_ref[k, pl.ds(i, 1), :] * prod[k * 128 : (k + 1) * 128]
    for shift in (-2, -1, 1, 2):
        place = i + shift
        inside = jnp.logical_and(place >= 0, place < 8)
        weight = jnp.where(inside, NEAR if abs(shift) == 1 else FAR, 0.0)
        place = jnp.clip(place, 0, 7)
        total = total + weight * both(w_ref, place, first, place)
    one = row_radius(i)
    two = col_radius((1, 128))
    lane = lax.broadcasted_iota(jnp.int32, (1, 128), 1)
    potential = (
        ang_ref[0] * (1.0 / (one * one))
        + ang_ref[1] * (1.0 / (two * two))
        + (CENTRE - 2.0 / one - 2.0 / two)
    )
    half = []
    for part in range(2):
        value = mine[:, part * 128 : (part + 1) * 128]
        near = jnp.where(lane >= 1, pltpu.roll(value, 1, 1), 0.0) + jnp.where(
            lane < 127, pltpu.roll(value, 127, 1), 0.0
        )
        far = jnp.where(lane >= 2, pltpu.roll(value, 2, 1), 0.0) + jnp.where(
            lane < 126, pltpu.roll(value, 126, 1), 0.0
        )
        half.append(
            total[:, part * 128 : (part + 1) * 128] + potential * value + NEAR * near + FAR * far
        )
    q_ref[0, 0] = natural(psi_ref, i, 0) + step * half[1]
    q_ref[0, 1] = natural(psi_ref, i, 1) - step * half[0]


def finish_kernel(first, last, step, q_ref, other_ref, h1_ref, h2_ref, d_ref, *refs):
    if last:
        out_ref, g_ref = refs
    else:
        out_ref, s1_ref, s2_ref, g_ref = refs
    i = pl.program_id(0)
    even = lax.rem(lax.axis_index("tile"), 2) == 0
    g_ref[...] = dipole_part(i, d_ref, both(other_ref, i, first, 0))
    low = i < 2
    high = i >= 6
    zero = jnp.float32(0.0)
    c0 = jnp.where(low, jnp.where(i == 0, FAR, zero), jnp.where(i == 6, FAR, NEAR))
    c1 = jnp.where(low, jnp.where(i == 0, NEAR, FAR), jnp.where(i == 6, zero, FAR))
    use1 = jnp.logical_or(jnp.logical_and(low, ~even), jnp.logical_and(high, even))
    use2 = jnp.logical_or(jnp.logical_and(low, even), jnp.logical_and(high, ~even))

    def halo(ref):
        for part in range(2):
            cols = pl.ds(part * 128, 128)
            g_ref[:, cols] += c0 * ref[0, part] + c1 * ref[1, part]

    @pl.when(use1)
    def _():
        halo(h1_ref)

    @pl.when(use2)
    def _():
        halo(h2_ref)

    real = q_ref[0, 0] + step * g_ref[:, 128:]
    imag = q_ref[0, 1] - step * g_ref[:, :128]
    if last:
        out_ref[pl.ds(i, 128, stride=16), :] = real
        out_ref[pl.ds(8 + i, 128, stride=16), :] = imag
        return
    out_ref[0, 0] = real
    out_ref[0, 1] = imag
    slot = jnp.where(low, i, i - 6)

    @pl.when(use1)
    def _():
        s1_ref[slot, 0] = real
        s1_ref[slot, 1] = imag

    @pl.when(use2)
    def _():
        s2_ref[slot, 0] = real
        s2_ref[slot, 1] = imag


FIELD = (8, 2, 128, 128)
EDGE = (2, 2, 128, 128)
FLAT = (2048, 128)


def shape(dims, dtype=F32):
    return jax.ShapeDtypeStruct(dims, dtype)


def local_call(first, step, w, other, psi, wcat, d, radial, ang):
    return pl.pallas_call(
        functools.partial(local_kernel, first, step),
        grid=(8,),
        in_specs=[
            whole(FLAT if first else FIELD),
            whole(FLAT) if first else row_spec(),
            whole(FLAT),
            whole((1024, 384)),
            whole((256, 384)),
            whole((8, 8, 256)),
            whole((2, 128, 128)),
        ],
        out_specs=row_spec(),
        out_shape=shape(FIELD),
        compiler_params=params(),
        cost_estimate=cost(2 * 2048 * 1280 * 384, 6 << 20),
        name="local",
    )(w, other, psi, wcat, d, radial, ang)


def finish_call(first, last, step, q, other, h1, h2, d):
    return pl.pallas_call(
        functools.partial(finish_kernel, first, last, step),
        grid=(8,),
        in_specs=[
            row_spec(),
            whole(FLAT) if first else row_spec(),
            whole(EDGE),
            whole(EDGE),
            whole((256, 384)),
        ],
        out_specs=[whole(FLAT)] if last else [row_spec(), whole(EDGE), whole(EDGE)],
        out_shape=[shape(FLAT)] if last else [shape(FIELD), shape(EDGE), shape(EDGE)],
        scratch_shapes=[pltpu.VMEM((128, 256), F32)],
        compiler_params=params(),
        cost_estimate=cost(2 * 2048 * 256 * 384, 4 << 20),
        name="finish",
    )(q, other, h1, h2, d)


def swaps(count, start):
    pairs = []
    for low in range(start, count - 1, 2):
        pairs += [(low, low + 1), (low + 1, low)]
    return pairs


def per_device(wavefunction, l_table, coupling, selection, dipole, field):
    blocks, tiles = lax.axis_size("lblk"), lax.axis_size("tile")
    psi = wavefunction.reshape(FLAT)
    inner = lambda value: lax.ppermute(value, "lblk", swaps(blocks, 0))
    outer = lambda value: lax.ppermute(value, "lblk", swaps(blocks, 1))
    edge1 = lambda value: lax.ppermute(value, "tile", swaps(tiles, 0))
    edge2 = lambda value: lax.ppermute(value, "tile", swaps(tiles, 1))

    below = lax.ppermute(dipole, "lblk", [(k, k + 1) for k in range(blocks - 1)])
    s1, s2 = pl.pallas_call(
        edges_kernel,
        in_specs=[whole(FLAT)],
        out_specs=[whole(EDGE)] * 2,
        out_shape=[shape(EDGE)] * 2,
        grid=(1,),
        compiler_params=params(),
        cost_estimate=cost(0, 2 << 20),
        name="edges",
    )(psi)
    wcat, radial, ang = pl.pallas_call(
        weights_kernel,
        grid=(1,),
        in_specs=[SCALAR, whole((1, 8, 128, 128)), whole((128, 2))],
        out_specs=[whole((1024, 384)), whole((8, 8, 256)), whole((2, 128, 128))],
        out_shape=[shape((1024, 384), BF16), shape((8, 8, 256)), shape((2, 128, 128))],
        compiler_params=params(),
        cost_estimate=cost(1 << 20, 2 << 20),
        name="weights",
    )(selection, coupling, l_table)
    d1, d2 = pl.pallas_call(
        dipole_kernel,
        grid=(1,),
        in_specs=[SCALAR, whole((1, 2, 128, 128)), whole((1, 2, 128, 128))],
        out_specs=[whole((256, 384))] * 2,
        out_shape=[shape((256, 384), BF16)] * 2,
        compiler_params=params(),
        cost_estimate=cost(1 << 20, 1 << 20),
        name="dipole",
    )(field, dipole, below)

    w = psi
    for order in range(TAYLOR, 0, -1):
        first, last = order == TAYLOR, order == 1
        step = time_step / order
        far = outer(w)
        h2 = edge2(s2)
        h1 = edge1(s1)
        near = inner(w)
        q = local_call(first, step, w, near, psi, wcat, d1, radial, ang)
        got = finish_call(first, last, step, q, far, h1, h2, d2)
        if last:
            return got[0].reshape(wavefunction.shape)
        w, s1, s2 = got


def solution(mesh):
    placed = (
        P("lblk", None, "tile", None),
        P("lblk", None),
        P("lblk", None, None, None),
        P("lblk", None),
        P("lblk", None, None, None),
        P(),
    )
    return jax.shard_map(
        per_device,
        mesh=mesh,
        in_specs=placed,
        out_specs=P("lblk", None, "tile", None),
        check_vma=False,
    )
```

profile of v0, /device:TPU:152, one launch (start us, length us, event | category | flops | bytes accessed | tf_op | source)
XLA Modules:
  0.0 173.3 jit_solution(8521938458360022963)
XLA Ops:
  0.0 3.9 %collective-permute-start.2 = (f32[2048,128]{1,0:T(8,128)}, f32[2048,128]{1,0:T(8,128)S(1)}, u32[]{:S(2)}, u32[]{:S(2)}) collective-permute-start(f32[2048,128]{1,0:T(8,128)} %bitcast.3), channel_id=1, source_target_pairs={{8,16},{16,8},{24,32},{32,24},{40,48},{48,40},{56,64},{64,56},{72,... | collective-permute-start | bytes 3145736 | tf_op jit(solution)/shard_map/ppermute | solution.py:285
  3.9 1.9 %collective-permute-start.1 = (f32[1,2,128,128]{3,2,1,0:T(8,128)}, f32[1,2,128,128]{3,2,1,0:T(8,128)S(1)}, u32[]{:S(2)}, u32[]{:S(2)}) collective-permute-start(f32[1,2,128,128]{3,2,1,0:T(8,128)} %own_ref.1), channel_id=1, source_target_pairs={{0,8},{8,16},{16,24},{24,32},{32,40},{40,48},{48,56},{56,64},{64,7... | collective-permute-start | bytes 393224 | tf_op jit(solution)/shard_map/ppermute | solution.py:289
  5.8 1.2 copy-done
  7.0 0.2 edges.1
  7.2 2.0 %collective-permute-start.3 = (f32[2,2,128,128]{3,2,1,0:T(8,128)S(1)}, f32[2,2,128,128]{3,2,1,0:T(8,128)S(1)}, u32[]{:S(2)}, u32[]{:S(2)}) collective-permute-start(f32[2,2,128,128]{3,2,1,0:T(8,128)S(1)} %get-tuple-element.25), channel_id=1, source_target_pairs={{0,1},{1,0},{2,3},{3,2},{4,5},{5,4},{6,7},{7,6},{8,9},{9,8},{10,11... | collective-permute-start | bytes 786440 | tf_op jit(solution)/shard_map/ppermute | solution.py:286
  9.2 2.2 %collective-permute-start.4 = (f32[2,2,128,128]{3,2,1,0:T(8,128)S(1)}, f32[2,2,128,128]{3,2,1,0:T(8,128)S(1)}, u32[]{:S(2)}, u32[]{:S(2)}) collective-permute-start(f32[2,2,128,128]{3,2,1,0:T(8,128)S(1)} %get-tuple-element.26), channel_id=1, source_target_pairs={{1,2},{2,1},{3,4},{4,3},{5,6},{6,5},{9,10},{10,9},{11,12},{12,11},... | collective-permute-start | bytes 786440 | tf_op jit(solution)/shard_map/ppermute | solution.py:287
  11.4 0.1 copy.7.l_ref
  12.2 1.0 copy-done.2
  13.3 0.8 weights.1
  14.1 26.1 %collective-permute-done.1.below_ref = f32[1,2,128,128]{3,2,1,0:T(8,128)S(1)} collective-permute-done((f32[1,2,128,128]{3,2,1,0:T(8,128)}, f32[1,2,128,128]{3,2,1,0:T(8,128)S(1)}, u32[]{:S(2)}, u32[]{:S(2)}) %collective-permute-start.1) | collective-permute-done | bytes 131104 | tf_op jit(solution)/shard_map/ppermute | solution.py:289
  40.1 0.2 dipole.1
  40.4 7.6 %local.4.q_ref = f32[8,2,128,128]{3,2,1,0:T(8,128)S(1)} custom-call(f32[2048,128]{1,0:T(8,128)S(1)} %bitcast.5, f32[2048,128]{1,0:T(8,128)} %collective-permute-done.other_ref, f32[2048,128]{1,0:T(8,128)S(1)} %bitcast.6, bf16[1024,384]{1,0:T(8,128)(2,1)S(1)} %get-tuple-element.21.wcat_ref, bf16[256,384]{1,0:T(8,128)(2,1)S(1)} %get-tuple-element.22.d_ref, ...), custom_call_target="tpu_custom_call" | custom-call | flops 2013265920 | bytes 6291456 | tf_op jit(solution)/shard_map/local/pallas_call | solution.py:234
  48.0 2.3 %finish.4 = (f32[8,2,128,128]{3,2,1,0:T(8,128)S(1)}, f32[2,2,128,128]{3,2,1,0:T(8,128)S(1)}, f32[2,2,128,128]{3,2,1,0:T(8,128)S(1)}) custom-call(f32[8,2,128,128]{3,2,1,0:T(8,128)S(1)} %local.4.q_ref, f32[2048,128]{1,0:T(8,128)S(1)} %collective-permute-done.2.other_ref, f32[2,2,128,128]{3,2,1,0:T(8,128)S(1)} %collective-permute-done.3.h1_ref, ...), custom_call_target="tpu_custom_call" | custom-call | flops 402653184 | bytes 4194304 | tf_op jit(solution)/shard_map/finish/pallas_call | solution.py:255
  50.5 1.9 %collective-permute-start.6 = (f32[8,2,128,128]{3,2,1,0:T(8,128)S(1)}, f32[8,2,128,128]{3,2,1,0:T(8,128)S(1)}, u32[]{:S(2)}, u32[]{:S(2)}) collective-permute-start(f32[8,2,128,128]{3,2,1,0:T(8,128)S(1)} %get-tuple-element.28.w_ref), channel_id=1, source_target_pairs={{8,16},{16,8},{24,32},{32,24},{40,48},{48,40},{56,64},{64,56},{72,... | collective-permute-start | bytes 3145736 | tf_op jit(solution)/shard_map/ppermute | solution.py:285
  52.5 4.1 %collective-permute-start.8 = (f32[2,2,128,128]{3,2,1,0:T(8,128)S(1)}, f32[2,2,128,128]{3,2,1,0:T(8,128)S(1)}, u32[]{:S(2)}, u32[]{:S(2)}) collective-permute-start(f32[2,2,128,128]{3,2,1,0:T(8,128)S(1)} %get-tuple-element.30), channel_id=1, source_target_pairs={{1,2},{2,1},{3,4},{4,3},{5,6},{6,5},{9,10},{10,9},{11,12},{12,11},... | collective-permute-start | bytes 786440 | tf_op jit(solution)/shard_map/ppermute | solution.py:287
  56.6 5.1 %local.5.q_ref = f32[8,2,128,128]{3,2,1,0:T(8,128)S(1)} custom-call(f32[8,2,128,128]{3,2,1,0:T(8,128)S(1)} %get-tuple-element.28.w_ref, f32[8,2,128,128]{3,2,1,0:T(8,128)S(1)} %collective-permute-done.5.other_ref, f32[2048,128]{1,0:T(8,128)S(1)} %bitcast.7, bf16[1024,384]{1,0:T(8,128)(2,1)S(1)} %get-tuple-element.21.wcat_ref, ...), custom_call_target="tpu_custom_call" | custom-call | flops 2013265920 | bytes 6291456 | tf_op jit(solution)/shard_map/local/pallas_call | solution.py:234
  61.7 16.6 %collective-permute-done.7.h1_ref = f32[2,2,128,128]{3,2,1,0:T(8,128)S(1)} collective-permute-done((f32[2,2,128,128]{3,2,1,0:T(8,128)S(1)}, f32[2,2,128,128]{3,2,1,0:T(8,128)S(1)}, u32[]{:S(2)}, u32[]{:S(2)}) %collective-permute-start.7) | collective-permute-done | bytes 262176 | tf_op jit(solution)/shard_map/ppermute | solution.py:286
  78.3 9.3 %collective-permute-done.8.h2_ref = f32[2,2,128,128]{3,2,1,0:T(8,128)S(1)} collective-permute-done((f32[2,2,128,128]{3,2,1,0:T(8,128)S(1)}, f32[2,2,128,128]{3,2,1,0:T(8,128)S(1)}, u32[]{:S(2)}, u32[]{:S(2)}) %collective-permute-start.8) | collective-permute-done | bytes 262176 | tf_op jit(solution)/shard_map/ppermute | solution.py:287
  87.7 2.1 %finish.5 = (f32[8,2,128,128]{3,2,1,0:T(8,128)S(1)}, f32[2,2,128,128]{3,2,1,0:T(8,128)S(1)}, f32[2,2,128,128]{3,2,1,0:T(8,128)S(1)}) custom-call(f32[8,2,128,128]{3,2,1,0:T(8,128)S(1)} %local.5.q_ref, f32[8,2,128,128]{3,2,1,0:T(8,128)S(1)} %collective-permute-done.6.other_ref, f32[2,2,128,128]{3,2,1,0:T(8,128)S(1)} %collective-permute-done.7.h1_ref, ...), custom_call_target="tpu_custom_call" | custom-call | flops 402653184 | bytes 4194304 | tf_op jit(solution)/shard_map/finish/pallas_call | solution.py:255
  89.9 7.4 %collective-permute-start.10 = (f32[8,2,128,128]{3,2,1,0:T(8,128)S(1)}, f32[8,2,128,128]{3,2,1,0:T(8,128)S(1)}, u32[]{:S(2)}, u32[]{:S(2)}) collective-permute-start(f32[8,2,128,128]{3,2,1,0:T(8,128)S(1)} %get-tuple-element.31.w_ref), channel_id=1, source_target_pairs={{8,16},{16,8},{24,32},{32,24},{40,48},{48,40},{56,64},{64,56},{72,... | collective-permute-start | bytes 3145736 | tf_op jit(solution)/shard_map/ppermute | solution.py:285
  97.5 5.0 %collective-permute-start.12 = (f32[2,2,128,128]{3,2,1,0:T(8,128)S(1)}, f32[2,2,128,128]{3,2,1,0:T(8,128)S(1)}, u32[]{:S(2)}, u32[]{:S(2)}) collective-permute-start(f32[2,2,128,128]{3,2,1,0:T(8,128)S(1)} %get-tuple-element.33), channel_id=1, source_target_pairs={{1,2},{2,1},{3,4},{4,3},{5,6},{6,5},{9,10},{10,9},{11,12},{12,11},... | collective-permute-start | bytes 786440 | tf_op jit(solution)/shard_map/ppermute | solution.py:287
  102.5 5.2 %local.6.q_ref = f32[8,2,128,128]{3,2,1,0:T(8,128)S(1)} custom-call(f32[8,2,128,128]{3,2,1,0:T(8,128)S(1)} %get-tuple-element.31.w_ref, f32[8,2,128,128]{3,2,1,0:T(8,128)S(1)} %collective-permute-done.9.other_ref, f32[2048,128]{1,0:T(8,128)S(1)} %bitcast.8, bf16[1024,384]{1,0:T(8,128)(2,1)S(1)} %get-tuple-element.21.wcat_ref, ...), custom_call_target="tpu_custom_call" | custom-call | flops 2013265920 | bytes 6291456 | tf_op jit(solution)/shard_map/local/pallas_call | solution.py:234
  107.6 10.9 %collective-permute-done.11.h1_ref = f32[2,2,128,128]{3,2,1,0:T(8,128)S(1)} collective-permute-done((f32[2,2,128,128]{3,2,1,0:T(8,128)S(1)}, f32[2,2,128,128]{3,2,1,0:T(8,128)S(1)}, u32[]{:S(2)}, u32[]{:S(2)}) %collective-permute-start.11) | collective-permute-done | bytes 262176 | tf_op jit(solution)/shard_map/ppermute | solution.py:286
  118.5 9.5 %collective-permute-done.12.h2_ref = f32[2,2,128,128]{3,2,1,0:T(8,128)S(1)} collective-permute-done((f32[2,2,128,128]{3,2,1,0:T(8,128)S(1)}, f32[2,2,128,128]{3,2,1,0:T(8,128)S(1)}, u32[]{:S(2)}, u32[]{:S(2)}) %collective-permute-start.12) | collective-permute-done | bytes 262176 | tf_op jit(solution)/shard_map/ppermute | solution.py:287
  128.0 2.6 %collective-permute-done.10.other_ref = f32[8,2,128,128]{3,2,1,0:T(8,128)S(1)} collective-permute-done((f32[8,2,128,128]{3,2,1,0:T(8,128)S(1)}, f32[8,2,128,128]{3,2,1,0:T(8,128)S(1)}, u32[]{:S(2)}, u32[]{:S(2)}) %collective-permute-start.10) | collective-permute-done | bytes 1048608 | tf_op jit(solution)/shard_map/ppermute | solution.py:285
  130.6 2.1 %finish.6 = (f32[8,2,128,128]{3,2,1,0:T(8,128)S(1)}, f32[2,2,128,128]{3,2,1,0:T(8,128)S(1)}, f32[2,2,128,128]{3,2,1,0:T(8,128)S(1)}) custom-call(f32[8,2,128,128]{3,2,1,0:T(8,128)S(1)} %local.6.q_ref, f32[8,2,128,128]{3,2,1,0:T(8,128)S(1)} %collective-permute-done.10.other_ref, f32[2,2,128,128]{3,2,1,0:T(8,128)S(1)} %collective-permute-done.11.h1_ref, ...), custom_call_target="tpu_custom_call" | custom-call | flops 402653184 | bytes 4194304 | tf_op jit(solution)/shard_map/finish/pallas_call | solution.py:255
  132.9 6.8 %collective-permute-start.14 = (f32[8,2,128,128]{3,2,1,0:T(8,128)S(1)}, f32[8,2,128,128]{3,2,1,0:T(8,128)S(1)}, u32[]{:S(2)}, u32[]{:S(2)}) collective-permute-start(f32[8,2,128,128]{3,2,1,0:T(8,128)S(1)} %get-tuple-element.34.w_ref), channel_id=1, source_target_pairs={{8,16},{16,8},{24,32},{32,24},{40,48},{48,40},{56,64},{64,56},{72,... | collective-permute-start | bytes 3145736 | tf_op jit(solution)/shard_map/ppermute | solution.py:285
  139.8 5.0 %collective-permute-start.16 = (f32[2,2,128,128]{3,2,1,0:T(8,128)S(1)}, f32[2,2,128,128]{3,2,1,0:T(8,128)S(1)}, u32[]{:S(2)}, u32[]{:S(2)}) collective-permute-start(f32[2,2,128,128]{3,2,1,0:T(8,128)S(1)} %get-tuple-element.36), channel_id=1, source_target_pairs={{1,2},{2,1},{3,4},{4,3},{5,6},{6,5},{9,10},{10,9},{11,12},{12,11},... | collective-permute-start | bytes 786440 | tf_op jit(solution)/shard_map/ppermute | solution.py:287
  144.8 5.2 %local.7.q_ref = f32[8,2,128,128]{3,2,1,0:T(8,128)S(1)} custom-call(f32[8,2,128,128]{3,2,1,0:T(8,128)S(1)} %get-tuple-element.34.w_ref, f32[8,2,128,128]{3,2,1,0:T(8,128)S(1)} %collective-permute-done.13.other_ref, f32[2048,128]{1,0:T(8,128)S(1)} %bitcast.9, bf16[1024,384]{1,0:T(8,128)(2,1)S(1)} %get-tuple-element.21.wcat_ref, ...), custom_call_target="tpu_custom_call" | custom-call | flops 2013265920 | bytes 6291456 | tf_op jit(solution)/shard_map/local/pallas_call | solution.py:234
  149.9 16.1 %collective-permute-done.15.h1_ref = f32[2,2,128,128]{3,2,1,0:T(8,128)S(1)} collective-permute-done((f32[2,2,128,128]{3,2,1,0:T(8,128)S(1)}, f32[2,2,128,128]{3,2,1,0:T(8,128)S(1)}, u32[]{:S(2)}, u32[]{:S(2)}) %collective-permute-start.15) | collective-permute-done | bytes 262176 | tf_op jit(solution)/shard_map/ppermute | solution.py:286
  166.0 3.8 %collective-permute-done.16.h2_ref = f32[2,2,128,128]{3,2,1,0:T(8,128)S(1)} collective-permute-done((f32[2,2,128,128]{3,2,1,0:T(8,128)S(1)}, f32[2,2,128,128]{3,2,1,0:T(8,128)S(1)}, u32[]{:S(2)}, u32[]{:S(2)}) %collective-permute-start.16) | collective-permute-done | bytes 262176 | tf_op jit(solution)/shard_map/ppermute | solution.py:287
  169.8 3.5 %finish.7 = f32[2048,128]{1,0:T(8,128)} custom-call(f32[8,2,128,128]{3,2,1,0:T(8,128)S(1)} %local.7.q_ref, f32[8,2,128,128]{3,2,1,0:T(8,128)S(1)} %collective-permute-done.14.other_ref, f32[2,2,128,128]{3,2,1,0:T(8,128)S(1)} %collective-permute-done.15.h1_ref, f32[2,2,128,128]{3,2,1,0:T(8,128)S(1)} %collective-permute-done.16.h2_ref, ...), custom_call_target="tpu_custom_call" | custom-call | flops 402653184 | bytes 4194304 | tf_op jit(solution)/shard_map/finish/pallas_call | solution.py:255
  (26 shorter events, 0.6 us)
Async XLA Ops:
  0.0 40.4 %collective-permute-start = (f32[2048,128]{1,0:T(8,128)}, f32[2048,128]{1,0:T(8,128)}, u32[]{:S(2)}, u32[]{:S(2)}) collective-permute-start(f32[2048,128]{1,0:T(8,128)} %bitcast.2), channel_id=1, source_target_pairs={{0,8},{8,0},{16,24},{24,16},{32,40},{40,32},{48,56},{56,48},{64,72... | collective-permute-start | bytes 3145736 | tf_op jit(solution)/shard_map/ppermute | solution.py:284
  0.0 48.0 %collective-permute-start.2 = (f32[2048,128]{1,0:T(8,128)}, f32[2048,128]{1,0:T(8,128)S(1)}, u32[]{:S(2)}, u32[]{:S(2)}) collective-permute-start(f32[2048,128]{1,0:T(8,128)} %bitcast.3), channel_id=1, source_target_pairs={{8,16},{16,8},{24,32},{32,24},{40,48},{48,40},{56,64},{64,56},{72,... | collective-permute-start | bytes 3145736 | tf_op jit(solution)/shard_map/ppermute | solution.py:285
  3.9 36.3 %collective-permute-start.1 = (f32[1,2,128,128]{3,2,1,0:T(8,128)}, f32[1,2,128,128]{3,2,1,0:T(8,128)S(1)}, u32[]{:S(2)}, u32[]{:S(2)}) collective-permute-start(f32[1,2,128,128]{3,2,1,0:T(8,128)} %own_ref.1), channel_id=1, source_target_pairs={{0,8},{8,16},{16,24},{24,32},{32,40},{40,48},{48,56},{56,64},{64,7... | collective-permute-start | bytes 393224 | tf_op jit(solution)/shard_map/ppermute | solution.py:289
  5.8 1.2 copy-start
  7.0 33.4 %copy-start.1 = (f32[128,2,8,128]{3,2,1,0:T(8,128)S(1)}, f32[128,2,8,128]{3,2,1,0:T(8,128)}, u32[]{:S(2)}) copy-start(f32[128,2,8,128]{3,2,1,0:T(8,128)} %param.6) | copy-start | bytes 3145732
  7.2 4.2 %copy-start.5 = (s32[128,2]{0,1:T(2,128)S(1)}, s32[128,2]{0,1:T(2,128)}, u32[]{:S(2)}) copy-start(s32[128,2]{0,1:T(2,128)} %param.7) | copy-start | bytes 3076
  7.2 40.8 %collective-permute-start.3 = (f32[2,2,128,128]{3,2,1,0:T(8,128)S(1)}, f32[2,2,128,128]{3,2,1,0:T(8,128)S(1)}, u32[]{:S(2)}, u32[]{:S(2)}) collective-permute-start(f32[2,2,128,128]{3,2,1,0:T(8,128)S(1)} %get-tuple-element.25), channel_id=1, source_target_pairs={{0,1},{1,0},{2,3},{3,2},{4,5},{5,4},{6,7},{7,6},{8,9},{9,8},{10,11... | collective-permute-start | bytes 786440 | tf_op jit(solution)/shard_map/ppermute | solution.py:286
  9.2 38.8 %collective-permute-start.4 = (f32[2,2,128,128]{3,2,1,0:T(8,128)S(1)}, f32[2,2,128,128]{3,2,1,0:T(8,128)S(1)}, u32[]{:S(2)}, u32[]{:S(2)}) collective-permute-start(f32[2,2,128,128]{3,2,1,0:T(8,128)S(1)} %get-tuple-element.26), channel_id=1, source_target_pairs={{1,2},{2,1},{3,4},{4,3},{5,6},{6,5},{9,10},{10,9},{11,12},{12,11},... | collective-permute-start | bytes 786440 | tf_op jit(solution)/shard_map/ppermute | solution.py:287
  11.5 0.7 copy-start.4
  12.2 1.0 copy-start.2
  13.3 26.9 %copy-start.3 = (f32[1,2,128,128]{3,2,1,0:T(8,128)S(1)}, f32[1,2,128,128]{3,2,1,0:T(8,128)}, u32[]{:S(2)}) copy-start(f32[1,2,128,128]{3,2,1,0:T(8,128)} %own_ref.1) | copy-start | bytes 393220
  50.4 6.2 %collective-permute-start.5 = (f32[8,2,128,128]{3,2,1,0:T(8,128)S(1)}, f32[8,2,128,128]{3,2,1,0:T(8,128)S(1)}, u32[]{:S(2)}, u32[]{:S(2)}) collective-permute-start(f32[8,2,128,128]{3,2,1,0:T(8,128)S(1)} %get-tuple-element.28.w_ref), channel_id=1, source_target_pairs={{0,8},{8,0},{16,24},{24,16},{32,40},{40,32},{48,56},{56,48},{64,72... | collective-permute-start | bytes 3145736 | tf_op jit(solution)/shard_map/ppermute | solution.py:284
  50.5 37.2 %collective-permute-start.6 = (f32[8,2,128,128]{3,2,1,0:T(8,128)S(1)}, f32[8,2,128,128]{3,2,1,0:T(8,128)S(1)}, u32[]{:S(2)}, u32[]{:S(2)}) collective-permute-start(f32[8,2,128,128]{3,2,1,0:T(8,128)S(1)} %get-tuple-element.28.w_ref), channel_id=1, source_target_pairs={{8,16},{16,8},{24,32},{32,24},{40,48},{48,40},{56,64},{64,56},{72,... | collective-permute-start | bytes 3145736 | tf_op jit(solution)/shard_map/ppermute | solution.py:285
  52.4 26.0 %collective-permute-start.7 = (f32[2,2,128,128]{3,2,1,0:T(8,128)S(1)}, f32[2,2,128,128]{3,2,1,0:T(8,128)S(1)}, u32[]{:S(2)}, u32[]{:S(2)}) collective-permute-start(f32[2,2,128,128]{3,2,1,0:T(8,128)S(1)} %get-tuple-element.29), channel_id=1, source_target_pairs={{0,1},{1,0},{2,3},{3,2},{4,5},{5,4},{6,7},{7,6},{8,9},{9,8},{10,11... | collective-permute-start | bytes 786440 | tf_op jit(solution)/shard_map/ppermute | solution.py:286
  52.5 35.2 %collective-permute-start.8 = (f32[2,2,128,128]{3,2,1,0:T(8,128)S(1)}, f32[2,2,128,128]{3,2,1,0:T(8,128)S(1)}, u32[]{:S(2)}, u32[]{:S(2)}) collective-permute-start(f32[2,2,128,128]{3,2,1,0:T(8,128)S(1)} %get-tuple-element.30), channel_id=1, source_target_pairs={{1,2},{2,1},{3,4},{4,3},{5,6},{6,5},{9,10},{10,9},{11,12},{12,11},... | collective-permute-start | bytes 786440 | tf_op jit(solution)/shard_map/ppermute | solution.py:287
  89.8 12.6 %collective-permute-start.9 = (f32[8,2,128,128]{3,2,1,0:T(8,128)S(1)}, f32[8,2,128,128]{3,2,1,0:T(8,128)S(1)}, u32[]{:S(2)}, u32[]{:S(2)}) collective-permute-start(f32[8,2,128,128]{3,2,1,0:T(8,128)S(1)} %get-tuple-element.31.w_ref), channel_id=1, source_target_pairs={{0,8},{8,0},{16,24},{24,16},{32,40},{40,32},{48,56},{56,48},{64,72... | collective-permute-start | bytes 3145736 | tf_op jit(solution)/shard_map/ppermute | solution.py:284
  89.9 40.7 %collective-permute-start.10 = (f32[8,2,128,128]{3,2,1,0:T(8,128)S(1)}, f32[8,2,128,128]{3,2,1,0:T(8,128)S(1)}, u32[]{:S(2)}, u32[]{:S(2)}) collective-permute-start(f32[8,2,128,128]{3,2,1,0:T(8,128)S(1)} %get-tuple-element.31.w_ref), channel_id=1, source_target_pairs={{8,16},{16,8},{24,32},{32,24},{40,48},{48,40},{56,64},{64,56},{72,... | collective-permute-start | bytes 3145736 | tf_op jit(solution)/shard_map/ppermute | solution.py:285
  97.4 21.2 %collective-permute-start.11 = (f32[2,2,128,128]{3,2,1,0:T(8,128)S(1)}, f32[2,2,128,128]{3,2,1,0:T(8,128)S(1)}, u32[]{:S(2)}, u32[]{:S(2)}) collective-permute-start(f32[2,2,128,128]{3,2,1,0:T(8,128)S(1)} %get-tuple-element.32), channel_id=1, source_target_pairs={{0,1},{1,0},{2,3},{3,2},{4,5},{5,4},{6,7},{7,6},{8,9},{9,8},{10,11... | collective-permute-start | bytes 786440 | tf_op jit(solution)/shard_map/ppermute | solution.py:286
  97.5 30.5 %collective-permute-start.12 = (f32[2,2,128,128]{3,2,1,0:T(8,128)S(1)}, f32[2,2,128,128]{3,2,1,0:T(8,128)S(1)}, u32[]{:S(2)}, u32[]{:S(2)}) collective-permute-start(f32[2,2,128,128]{3,2,1,0:T(8,128)S(1)} %get-tuple-element.33), channel_id=1, source_target_pairs={{1,2},{2,1},{3,4},{4,3},{5,6},{6,5},{9,10},{10,9},{11,12},{12,11},... | collective-permute-start | bytes 786440 | tf_op jit(solution)/shard_map/ppermute | solution.py:287
  132.8 12.0 %collective-permute-start.13 = (f32[8,2,128,128]{3,2,1,0:T(8,128)S(1)}, f32[8,2,128,128]{3,2,1,0:T(8,128)S(1)}, u32[]{:S(2)}, u32[]{:S(2)}) collective-permute-start(f32[8,2,128,128]{3,2,1,0:T(8,128)S(1)} %get-tuple-element.34.w_ref), channel_id=1, source_target_pairs={{0,8},{8,0},{16,24},{24,16},{32,40},{40,32},{48,56},{56,48},{64,72... | collective-permute-start | bytes 3145736 | tf_op jit(solution)/shard_map/ppermute | solution.py:284
  132.9 37.0 %collective-permute-start.14 = (f32[8,2,128,128]{3,2,1,0:T(8,128)S(1)}, f32[8,2,128,128]{3,2,1,0:T(8,128)S(1)}, u32[]{:S(2)}, u32[]{:S(2)}) collective-permute-start(f32[8,2,128,128]{3,2,1,0:T(8,128)S(1)} %get-tuple-element.34.w_ref), channel_id=1, source_target_pairs={{8,16},{16,8},{24,32},{32,24},{40,48},{48,40},{56,64},{64,56},{72,... | collective-permute-start | bytes 3145736 | tf_op jit(solution)/shard_map/ppermute | solution.py:285
  139.7 26.3 %collective-permute-start.15 = (f32[2,2,128,128]{3,2,1,0:T(8,128)S(1)}, f32[2,2,128,128]{3,2,1,0:T(8,128)S(1)}, u32[]{:S(2)}, u32[]{:S(2)}) collective-permute-start(f32[2,2,128,128]{3,2,1,0:T(8,128)S(1)} %get-tuple-element.35), channel_id=1, source_target_pairs={{0,1},{1,0},{2,3},{3,2},{4,5},{5,4},{6,7},{7,6},{8,9},{9,8},{10,11... | collective-permute-start | bytes 786440 | tf_op jit(solution)/shard_map/ppermute | solution.py:286
  139.8 30.1 %collective-permute-start.16 = (f32[2,2,128,128]{3,2,1,0:T(8,128)S(1)}, f32[2,2,128,128]{3,2,1,0:T(8,128)S(1)}, u32[]{:S(2)}, u32[]{:S(2)}) collective-permute-start(f32[2,2,128,128]{3,2,1,0:T(8,128)S(1)} %get-tuple-element.36), channel_id=1, source_target_pairs={{1,2},{2,1},{3,4},{4,3},{5,6},{6,5},{9,10},{10,9},{11,12},{12,11},... | collective-permute-start | bytes 786440 | tf_op jit(solution)/shard_map/ppermute | solution.py:287
where the time goes:
time: 174 us; the launch traced here: 173 us
  waiting for transfers between devices  94.9 us (55%)
  starting transfers between devices  40.7 us (23%)
  Pallas kernels  34.3 us (20%)
  local copies, waits for them, and re-layouts  2.39 us (1%)
    ppermute x4, waiting for transfers between devices, per_device(): edge1 = lambda value: lax.ppermute(value, 'tile', swaps(tiles, 0))  43.6 us
    ppermute x1, waiting for transfers between devices, per_device(): lax.ppermute(dipole, 'lblk', [(k, k + 1) for k in range(blocks - 1)])  26.1 us
    pallas_call x4, Pallas kernels, local_call(): pl.pallas_call(functools.partial(local_kernel, first, step), grid=(8,), i...  23 us
    ppermute x4, waiting for transfers between devices, per_device(): edge2 = lambda value: lax.ppermute(value, 'tile', swaps(tiles, 1))  22.6 us
    ppermute x4, starting transfers between devices, per_device(): outer = lambda value: lax.ppermute(value, 'lblk', swaps(blocks, 1))  20 us
    ppermute x4, starting transfers between devices, per_device(): edge2 = lambda value: lax.ppermute(value, 'tile', swaps(tiles, 1))  16.3 us
    pallas_call x4, Pallas kernels, finish_call(): pl.pallas_call(functools.partial(finish_kernel, first, last, step), grid=...  10.1 us
  transfers between devices with their start and end apart: 17, of which 8 were waited for; matrix products, arithmetic and copies ran while one was open for 0% of the time, Pallas kernels for 14%

commit v1 on v0

--- a/solution.py
+++ b/solution.py
@@ -7,8 +7,10 @@
 from jax.experimental.pallas import tpu as pltpu
 from jax.sharding import PartitionSpec as P
 
+
 NMP = 8
 TAYLOR = 4
+STRAIGHT = 5
 
 time_step = 0.03
 grid_step = 0.5
@@ -57,13 +59,11 @@
     return radius_start + grid_step * col.astype(F32)
 
 
-def natural(ref, i, part):
-    return ref[pl.ds(part * 8 + i, 128, stride=16), :]
-
-
-def both(ref, i, first, row):
-    if first:
-        return jnp.concatenate([natural(ref, i, 0), natural(ref, i, 1)], axis=1)
+def natural(ref, i, part, count=128):
+    return ref[pl.ds(part * 8 + i, count, stride=16), :]
+
+
+def both(ref, row):
     return jnp.concatenate([ref[row, 0], ref[row, 1]], axis=1)
 
 
@@ -77,16 +77,21 @@
     return jnp.concatenate([high, high, low], axis=1)
 
 
-def edges_kernel(psi_ref, h1_ref, h2_ref):
+def unpack_kernel(psi_ref, w_ref, fa_ref, fb_ref, s1_ref, s2_ref):
     even = lax.rem(lax.axis_index("tile"), 2) == 0
-
-    def store(ref, start):
-        for row in range(2):
-            for part in range(2):
-                ref[row, part] = natural(psi_ref, start + row, part)
-
-    store(h1_ref, jnp.where(even, 6, 0))
-    store(h2_ref, jnp.where(even, 0, 6))
+    for row in range(8):
+        for part in range(2):
+            value = natural(psi_ref, row, part)
+            w_ref[row, part] = value
+            if row < STRAIGHT:
+                fa_ref[row, part] = value
+            else:
+                fb_ref[row - STRAIGHT, part] = value
+    for row in range(2):
+        for part in range(2):
+            low, high = w_ref[row, part], w_ref[6 + row, part]
+            s1_ref[row, part] = jnp.where(even, high, low)
+            s2_ref[row, part] = jnp.where(even, low, high)
 
 
 def weights_kernel(sel_ref, coup_ref, l_ref, wcat_ref, radial_ref, ang_ref):
@@ -134,11 +139,11 @@
     return row_radius(i) * out[:128] + col_radius((1, 256)) * out[128:]
 
 
-def local_kernel(first, step, w_ref, other_ref, psi_ref, wcat_ref, d_ref, radial_ref, ang_ref, q_ref):
+def local_kernel(step, w_ref, other_ref, psi_ref, wcat_ref, d_ref, radial_ref, ang_ref, q_ref):
     i = pl.program_id(0)
-    mine = both(w_ref, i, first, i)
+    mine = both(w_ref, i)
     prod = jnp.dot(wcat_ref[...], operand(mine), preferred_element_type=F32)
-    total = dipole_part(i, d_ref, both(other_ref, i, first, 0))
+    total = dipole_part(i, d_ref, both(other_ref, 0))
     for k in range(NMP):
         total = total + radial_ref[k, pl.ds(i, 1), :] * prod[k * 128 : (k + 1) * 128]
     for shift in (-2, -1, 1, 2):
@@ -146,7 +151,7 @@
         inside = jnp.logical_and(place >= 0, place < 8)
         weight = jnp.where(inside, NEAR if abs(shift) == 1 else FAR, 0.0)
         place = jnp.clip(place, 0, 7)
-        total = total + weight * both(w_ref, place, first, place)
+        total = total + weight * both(w_ref, place)
     one = row_radius(i)
     two = col_radius((1, 128))
     lane = lax.broadcasted_iota(jnp.int32, (1, 128), 1)
@@ -171,14 +176,26 @@
     q_ref[0, 1] = natural(psi_ref, i, 1) - step * half[0]
 
 
-def finish_kernel(first, last, step, q_ref, other_ref, h1_ref, h2_ref, d_ref, *refs):
+def far_row(i, ra_ref, rb_ref, rc_ref):
+    place = lax.rem(lax.axis_index("lblk"), 8)
+    relayed = jnp.logical_or(place == 0, place == 7)
+    parts = [
+        jnp.where(
+            i < STRAIGHT, ra_ref[0, part], jnp.where(relayed, rc_ref[0, part], rb_ref[0, part])
+        )
+        for part in range(2)
+    ]
+    return jnp.concatenate(parts, axis=1)
+
+
+def finish_kernel(last, step, q_ref, ra_ref, rb_ref, rc_ref, h1_ref, h2_ref, d_ref, *refs):
     if last:
         out_ref, g_ref = refs
     else:
-        out_ref, s1_ref, s2_ref, g_ref = refs
+        out_ref, fa_ref, fb_ref, s1_ref, s2_ref, g_ref = refs
     i = pl.program_id(0)
     even = lax.rem(lax.axis_index("tile"), 2) == 0
-    g_ref[...] = dipole_part(i, d_ref, both(other_ref, i, first, 0))
+    g_ref[...] = dipole_part(i, d_ref, far_row(i, ra_ref, rb_ref, rc_ref))
     low = i < 2
     high = i >= 6
     zero = jnp.float32(0.0)
@@ -206,37 +223,37 @@
         out_ref[pl.ds(i, 128, stride=16), :] = real
         out_ref[pl.ds(8 + i, 128, stride=16), :] = imag
         return
-    out_ref[0, 0] = real
-    out_ref[0, 1] = imag
+
+    def store(ref, row):
+        ref[row, 0] = real
+        ref[row, 1] = imag
+
     slot = jnp.where(low, i, i - 6)
-
-    @pl.when(use1)
-    def _():
-        s1_ref[slot, 0] = real
-        s1_ref[slot, 1] = imag
-
-    @pl.when(use2)
-    def _():
-        s2_ref[slot, 0] = real
-        s2_ref[slot, 1] = imag
+    store(out_ref, 0)
+    pl.when(i < STRAIGHT)(lambda: store(fa_ref, 0))
+    pl.when(i >= STRAIGHT)(lambda: store(fb_ref, 0))
+    pl.when(use1)(lambda: store(s1_ref, slot))
+    pl.when(use2)(lambda: store(s2_ref, slot))
 
 
 FIELD = (8, 2, 128, 128)
 EDGE = (2, 2, 128, 128)
 FLAT = (2048, 128)
+EARLY = (STRAIGHT, 2, 128, 128)
+LATE = (8 - STRAIGHT, 2, 128, 128)
 
 
 def shape(dims, dtype=F32):
     return jax.ShapeDtypeStruct(dims, dtype)
 
 
-def local_call(first, step, w, other, psi, wcat, d, radial, ang):
+def local_call(step, w, other, psi, wcat, d, radial, ang):
     return pl.pallas_call(
-        functools.partial(local_kernel, first, step),
+        functools.partial(local_kernel, step),
         grid=(8,),
         in_specs=[
-            whole(FLAT if first else FIELD),
-            whole(FLAT) if first else row_spec(),
+            whole(FIELD),
+            row_spec(),
             whole(FLAT),
             whole((1024, 384)),
             whole((256, 384)),
@@ -251,24 +268,39 @@
     )(w, other, psi, wcat, d, radial, ang)
 
 
-def finish_call(first, last, step, q, other, h1, h2, d):
+def early_rows():
+    return pl.BlockSpec((1, 2, 128, 128), lambda i: (jnp.minimum(i, STRAIGHT - 1), 0, 0, 0))
+
+
+def late_rows():
+    return pl.BlockSpec((1, 2, 128, 128), lambda i: (jnp.maximum(i - STRAIGHT, 0), 0, 0, 0))
+
+
+SENT = [FIELD, EARLY, LATE, EDGE, EDGE]
+
+
+def finish_call(last, step, q, ra, rb, rc, h1, h2, d):
     return pl.pallas_call(
-        functools.partial(finish_kernel, first, last, step),
+        functools.partial(finish_kernel, last, step),
         grid=(8,),
         in_specs=[
             row_spec(),
-            whole(FLAT) if first else row_spec(),
+            early_rows(),
+            late_rows(),
+            late_rows(),
             whole(EDGE),
             whole(EDGE),
             whole((256, 384)),
         ],
-        out_specs=[whole(FLAT)] if last else [row_spec(), whole(EDGE), whole(EDGE)],
-        out_shape=[shape(FLAT)] if last else [shape(FIELD), shape(EDGE), shape(EDGE)],
+        out_specs=[whole(FLAT)]
+        if last
+        else [row_spec(), early_rows(), late_rows(), whole(EDGE), whole(EDGE)],
+        out_shape=[shape(dims) for dims in ([FLAT] if last else SENT)],
         scratch_shapes=[pltpu.VMEM((128, 256), F32)],
         compiler_params=params(),
         cost_estimate=cost(2 * 2048 * 256 * 384, 4 << 20),
         name="finish",
-    )(q, other, h1, h2, d)
+    )(q, ra, rb, rc, h1, h2, d)
 
 
 def swaps(count, start):
@@ -278,24 +310,34 @@
     return pairs
 
 
+def relay_pairs(blocks):
+    pairs = []
+    for low in range(1, blocks - 1, 2):
+        if low % 8 == 7:
+            pairs += [(low, low - 7), (low + 1, low + 8)]
+        else:
+            pairs += [(low, low + 1), (low + 1, low)]
+    onward = []
+    for low in range(7, blocks - 1, 8):
+        onward += [(low - 7, low + 1), (low + 8, low)]
+    return pairs, onward
+
+
 def per_device(wavefunction, l_table, coupling, selection, dipole, field):
     blocks, tiles = lax.axis_size("lblk"), lax.axis_size("tile")
     psi = wavefunction.reshape(FLAT)
-    inner = lambda value: lax.ppermute(value, "lblk", swaps(blocks, 0))
-    outer = lambda value: lax.ppermute(value, "lblk", swaps(blocks, 1))
-    edge1 = lambda value: lax.ppermute(value, "tile", swaps(tiles, 0))
-    edge2 = lambda value: lax.ppermute(value, "tile", swaps(tiles, 1))
+    relay, onward = relay_pairs(blocks)
 
     below = lax.ppermute(dipole, "lblk", [(k, k + 1) for k in range(blocks - 1)])
-    s1, s2 = pl.pallas_call(
-        edges_kernel,
+    w, fa, fb, s1, s2 = pl.pallas_call(
+        unpack_kernel,
         in_specs=[whole(FLAT)],
-        out_specs=[whole(EDGE)] * 2,
-        out_shape=[shape(EDGE)] * 2,
+        out_specs=[whole(dims) for dims in SENT],
+        out_shape=[shape(dims) for dims in SENT],
         grid=(1,),
         compiler_params=params(),
-        cost_estimate=cost(0, 2 << 20),
-        name="edges",
+        cost_estimate=cost(0, 4 << 20),
+        name="unpack",
     )(psi)
     wcat, radial, ang = pl.pallas_call(
         weights_kernel,
@@ -318,19 +360,20 @@
         name="dipole",
     )(field, dipole, below)
 
-    w = psi
     for order in range(TAYLOR, 0, -1):
-        first, last = order == TAYLOR, order == 1
+        last = order == 1
         step = time_step / order
-        far = outer(w)
-        h2 = edge2(s2)
-        h1 = edge1(s1)
-        near = inner(w)
-        q = local_call(first, step, w, near, psi, wcat, d1, radial, ang)
-        got = finish_call(first, last, step, q, far, h1, h2, d2)
+        ra = lax.ppermute(fa, "lblk", swaps(blocks, 1))
+        rb = lax.ppermute(fb, "lblk", relay)
+        h2 = lax.ppermute(s2, "tile", swaps(tiles, 1))
+        h1 = lax.ppermute(s1, "tile", swaps(tiles, 0))
+        near = lax.ppermute(w, "lblk", swaps(blocks, 0))
+        rc = lax.ppermute(rb, "lblk", onward)
+        q = local_call(step, w, near, psi, wcat, d1, radial, ang)
+        got = finish_call(last, step, q, ra, rb, rc, h1, h2, d2)
         if last:
             return got[0].reshape(wavefunction.shape)
-        w, s1, s2 = got
+        w, fa, fb, s1, s2 = got
 
 
 def solution(mesh):

time: 174 us -> 165 us (0.948)
  waiting for transfers between devices: 94.9 us -> 73.1 us
  starting transfers between devices: 40.7 us -> 50.1 us
  Pallas kernels: 34.3 us -> 36.2 us
    ppermute x16 -> x24, waiting for transfers between devices: 68.8 us -> 52.2 us  [the longest x4 18 us: per_device(): rb = lax.ppermute(fb, 'lblk', relay)]
    ppermute x16 -> x24, starting transfers between devices: 38.8 us -> 48.2 us  [the longest x4 16.5 us: per_device(): h2 = lax.ppermute(s2, 'tile', swaps(tiles, 1))]
    ppermute x1, waiting for transfers between devices: 26.1 us -> 20.9 us  [per_device(): lax.ppermute(dipole, 'lblk', [(k, k + 1) for k in range(blocks - 1)])]
    pallas_call x9, Pallas kernels: 33.3 us -> 35.2 us  [the longest x4 22.7 us: local_call(): pl.pallas_call(functools.partial(local_kernel, step), grid=(8,), in_specs...]
  transfers between devices with their start and end apart: 17 -> 25, of which waited for: 8 -> 11; matrix products, arithmetic and copies ran while one was open for 0% -> 0% of each run, Pallas kernels for 14% -> 15%
where the time goes in v1:
time: 165 us; the launch traced here: 163 us
  waiting for transfers between devices  73.1 us (44%)
  starting transfers between devices  50.1 us (30%)
  Pallas kernels  36.2 us (22%)
  local copies, waits for them, and re-layouts  3.03 us (2%)
    pallas_call x4, Pallas kernels, local_call(): pl.pallas_call(functools.partial(local_kernel, step), grid=(8,), in_specs...  22.7 us
    ppermute x1, waiting for transfers between devices, per_device(): lax.ppermute(dipole, 'lblk', [(k, k + 1) for k in range(blocks - 1)])  20.9 us
    ppermute x4, waiting for transfers between devices, per_device(): rb = lax.ppermute(fb, 'lblk', relay)  18 us
    ppermute x4, waiting for transfers between devices, per_device(): h2 = lax.ppermute(s2, 'tile', swaps(tiles, 1))  17.4 us
    ppermute x4, waiting for transfers between devices, per_device(): h1 = lax.ppermute(s1, 'tile', swaps(tiles, 0))  16.7 us
    ppermute x4, starting transfers between devices, per_device(): h2 = lax.ppermute(s2, 'tile', swaps(tiles, 1))  16.5 us
    pallas_call x4, Pallas kernels, finish_call(): pl.pallas_call(functools.partial(finish_kernel, last, step), grid=(8,), i...  11 us
    ppermute x4, starting transfers between devices, per_device(): ra = lax.ppermute(fa, 'lblk', swaps(blocks, 1))  10.7 us
  transfers between devices with their start and end apart: 25, of which 11 were waited for; matrix products, arithmetic and copies ran while one was open for 0% of the time, Pallas kernels for 15%

profile of v1, /device:TPU:152, one launch (start us, length us, event | category | flops | bytes accessed | tf_op | source)
XLA Modules:
  0.0 163.5 jit_solution(17153308383281858254)
XLA Ops:
  2.7 4.8 %collective-permute-start.3 = (f32[3,2,128,128]{3,2,1,0:T(8,128)S(1)}, f32[3,2,128,128]{3,2,1,0:T(8,128)S(1)}, u32[]{:S(2)}, u32[]{:S(2)}) collective-permute-start(f32[3,2,128,128]{3,2,1,0:T(8,128)S(1)} %get-tuple-element.36), channel_id=1, source_target_pairs={{8,16},{16,8},{24,32},{32,24},{40,48},{48,40},{56,0},{64,120},{72,... | collective-permute-start | bytes 1179656 | tf_op jit(solution)/shard_map/ppermute | solution.py:367
  7.5 1.9 %collective-permute-start.2 = (f32[5,2,128,128]{3,2,1,0:T(8,128)}, f32[5,2,128,128]{3,2,1,0:T(8,128)S(1)}, u32[]{:S(2)}, u32[]{:S(2)}) collective-permute-start(f32[5,2,128,128]{3,2,1,0:T(8,128)} %get-tuple-element.35), channel_id=1, source_target_pairs={{8,16},{16,8},{24,32},{32,24},{40,48},{48,40},{56,64},{64,56},{72,... | collective-permute-start | bytes 1966088 | tf_op jit(solution)/shard_map/ppermute | solution.py:366
  9.4 1.9 %collective-permute-start.1 = (f32[1,2,128,128]{3,2,1,0:T(8,128)}, f32[1,2,128,128]{3,2,1,0:T(8,128)S(1)}, u32[]{:S(2)}, u32[]{:S(2)}) collective-permute-start(f32[1,2,128,128]{3,2,1,0:T(8,128)} %own_ref.1), channel_id=1, source_target_pairs={{0,8},{8,16},{16,24},{24,32},{32,40},{40,48},{48,56},{56,64},{64,7... | collective-permute-start | bytes 393224 | tf_op jit(solution)/shard_map/ppermute | solution.py:331
  13.0 3.1 %collective-permute-start.4 = (f32[3,2,128,128]{3,2,1,0:T(8,128)S(1)}, f32[3,2,128,128]{3,2,1,0:T(8,128)S(1)}, u32[]{:S(2)}, u32[]{:S(2)}) collective-permute-start(f32[3,2,128,128]{3,2,1,0:T(8,128)S(1)} %collective-permute-done.3.rb_ref), channel_id=1, source_target_pairs={{0,64},{120,56},{64,128},{184,120},{128,192},{248,184},{1,65},{121... | collective-permute-start | bytes 1179656 | tf_op jit(solution)/shard_map/ppermute | solution.py:371
  17.2 20.9 %collective-permute-done.1.below_ref = f32[1,2,128,128]{3,2,1,0:T(8,128)S(1)} collective-permute-done((f32[1,2,128,128]{3,2,1,0:T(8,128)}, f32[1,2,128,128]{3,2,1,0:T(8,128)S(1)}, u32[]{:S(2)}, u32[]{:S(2)}) %collective-permute-start.1) | collective-permute-done | bytes 131104 | tf_op jit(solution)/shard_map/ppermute | solution.py:331
  38.2 2.0 %collective-permute-start.6 = (f32[2,2,128,128]{3,2,1,0:T(8,128)S(1)}, f32[2,2,128,128]{3,2,1,0:T(8,128)S(1)}, u32[]{:S(2)}, u32[]{:S(2)}) collective-permute-start(f32[2,2,128,128]{3,2,1,0:T(8,128)S(1)} %get-tuple-element.38), channel_id=1, source_target_pairs={{1,2},{2,1},{3,4},{4,3},{5,6},{6,5},{9,10},{10,9},{11,12},{12,11},... | collective-permute-start | bytes 786440 | tf_op jit(solution)/shard_map/ppermute | solution.py:368
  43.7 7.3 %local.4.q_ref = f32[8,2,128,128]{3,2,1,0:T(8,128)S(1)} custom-call(f32[8,2,128,128]{3,2,1,0:T(8,128)} %get-tuple-element.30.w_ref, f32[8,2,128,128]{3,2,1,0:T(8,128)} %collective-permute-done.other_ref, f32[2048,128]{1,0:T(8,128)S(1)} %bitcast.3, bf16[1024,384]{1,0:T(8,128)(2,1)S(1)} %get-tuple-element.31.wcat_ref, ...), custom_call_target="tpu_custom_call" | custom-call | flops 2013265920 | bytes 6291456 | tf_op jit(solution)/shard_map/local/pallas_call | solution.py:251
  51.1 2.5 %finish.4 = (f32[8,2,128,128]{3,2,1,0:T(8,128)S(1)}, f32[5,2,128,128]{3,2,1,0:T(8,128)S(1)}, f32[3,2,128,128]{3,2,1,0:T(8,128)S(1)}, f32[2,2,128,128]{3,2,1,0:T(8,128)S(1)}, f32[2,2,128,128]{3,2,1,0:T(8,128)S(1)}) custom-call(f32[8,2,128,128]{3,2,1,0:T(8,128)S(1)} %local.4.q_ref, f32[5,2,128,128]{3,2,1,0:T(8,128)S(1)} %collective-permute-done.2.ra_ref, ...), custom_call_target="tpu_custom_call" | custom-call | flops 402653184 | bytes 4194304 | tf_op jit(solution)/shard_map/finish/pallas_call | solution.py:283
  53.7 1.9 %collective-permute-start.9 = (f32[3,2,128,128]{3,2,1,0:T(8,128)S(1)}, f32[3,2,128,128]{3,2,1,0:T(8,128)S(1)}, u32[]{:S(2)}, u32[]{:S(2)}) collective-permute-start(f32[3,2,128,128]{3,2,1,0:T(8,128)S(1)} %get-tuple-element.42), channel_id=1, source_target_pairs={{8,16},{16,8},{24,32},{32,24},{40,48},{48,40},{56,0},{64,120},{72,... | collective-permute-start | bytes 1179656 | tf_op jit(solution)/shard_map/ppermute | solution.py:367
  55.6 1.9 %collective-permute-start.8 = (f32[5,2,128,128]{3,2,1,0:T(8,128)S(1)}, f32[5,2,128,128]{3,2,1,0:T(8,128)S(1)}, u32[]{:S(2)}, u32[]{:S(2)}) collective-permute-start(f32[5,2,128,128]{3,2,1,0:T(8,128)S(1)} %get-tuple-element.41), channel_id=1, source_target_pairs={{8,16},{16,8},{24,32},{32,24},{40,48},{48,40},{56,64},{64,56},{72,... | collective-permute-start | bytes 1966088 | tf_op jit(solution)/shard_map/ppermute | solution.py:366
  57.5 6.4 %collective-permute-done.9.rb_ref = f32[3,2,128,128]{3,2,1,0:T(8,128)S(1)} collective-permute-done((f32[3,2,128,128]{3,2,1,0:T(8,128)S(1)}, f32[3,2,128,128]{3,2,1,0:T(8,128)S(1)}, u32[]{:S(2)}, u32[]{:S(2)}) %collective-permute-start.9) | collective-permute-done | bytes 393248 | tf_op jit(solution)/shard_map/ppermute | solution.py:367
  66.0 4.8 %collective-permute-start.12 = (f32[2,2,128,128]{3,2,1,0:T(8,128)S(1)}, f32[2,2,128,128]{3,2,1,0:T(8,128)S(1)}, u32[]{:S(2)}, u32[]{:S(2)}) collective-permute-start(f32[2,2,128,128]{3,2,1,0:T(8,128)S(1)} %get-tuple-element.44), channel_id=1, source_target_pairs={{1,2},{2,1},{3,4},{4,3},{5,6},{6,5},{9,10},{10,9},{11,12},{12,11},... | collective-permute-start | bytes 786440 | tf_op jit(solution)/shard_map/ppermute | solution.py:368
  70.8 5.2 %local.5.q_ref = f32[8,2,128,128]{3,2,1,0:T(8,128)S(1)} custom-call(f32[8,2,128,128]{3,2,1,0:T(8,128)S(1)} %get-tuple-element.40.w_ref, f32[8,2,128,128]{3,2,1,0:T(8,128)S(1)} %collective-permute-done.7.other_ref, f32[2048,128]{1,0:T(8,128)S(1)} %bitcast.4, bf16[1024,384]{1,0:T(8,128)(2,1)S(1)} %get-tuple-element.31.wcat_ref, ...), custom_call_target="tpu_custom_call" | custom-call | flops 2013265920 | bytes 6291456 | tf_op jit(solution)/shard_map/local/pallas_call | solution.py:251
  76.0 5.6 %collective-permute-done.11.h1_ref = f32[2,2,128,128]{3,2,1,0:T(8,128)S(1)} collective-permute-done((f32[2,2,128,128]{3,2,1,0:T(8,128)S(1)}, f32[2,2,128,128]{3,2,1,0:T(8,128)S(1)}, u32[]{:S(2)}, u32[]{:S(2)}) %collective-permute-start.11) | collective-permute-done | bytes 262176 | tf_op jit(solution)/shard_map/ppermute | solution.py:369
  81.6 5.7 %collective-permute-done.12.h2_ref = f32[2,2,128,128]{3,2,1,0:T(8,128)S(1)} collective-permute-done((f32[2,2,128,128]{3,2,1,0:T(8,128)S(1)}, f32[2,2,128,128]{3,2,1,0:T(8,128)S(1)}, u32[]{:S(2)}, u32[]{:S(2)}) %collective-permute-start.12) | collective-permute-done | bytes 262176 | tf_op jit(solution)/shard_map/ppermute | solution.py:368
  87.3 2.5 %finish.5 = (f32[8,2,128,128]{3,2,1,0:T(8,128)S(1)}, f32[5,2,128,128]{3,2,1,0:T(8,128)S(1)}, f32[3,2,128,128]{3,2,1,0:T(8,128)S(1)}, f32[2,2,128,128]{3,2,1,0:T(8,128)S(1)}, f32[2,2,128,128]{3,2,1,0:T(8,128)S(1)}) custom-call(f32[8,2,128,128]{3,2,1,0:T(8,128)S(1)} %local.5.q_ref, f32[5,2,128,128]{3,2,1,0:T(8,128)S(1)} %collective-permute-done.8.ra_ref, ...), custom_call_target="tpu_custom_call" | custom-call | flops 402653184 | bytes 4194304 | tf_op jit(solution)/shard_map/finish/pallas_call | solution.py:283
  89.9 1.9 %collective-permute-start.15 = (f32[3,2,128,128]{3,2,1,0:T(8,128)S(1)}, f32[3,2,128,128]{3,2,1,0:T(8,128)S(1)}, u32[]{:S(2)}, u32[]{:S(2)}) collective-permute-start(f32[3,2,128,128]{3,2,1,0:T(8,128)S(1)} %get-tuple-element.47), channel_id=1, source_target_pairs={{8,16},{16,8},{24,32},{32,24},{40,48},{48,40},{56,0},{64,120},{72,... | collective-permute-start | bytes 1179656 | tf_op jit(solution)/shard_map/ppermute | solution.py:367
  91.8 3.9 %collective-permute-start.14 = (f32[5,2,128,128]{3,2,1,0:T(8,128)S(1)}, f32[5,2,128,128]{3,2,1,0:T(8,128)S(1)}, u32[]{:S(2)}, u32[]{:S(2)}) collective-permute-start(f32[5,2,128,128]{3,2,1,0:T(8,128)S(1)} %get-tuple-element.46), channel_id=1, source_target_pairs={{8,16},{16,8},{24,32},{32,24},{40,48},{48,40},{56,64},{64,56},{72,... | collective-permute-start | bytes 1966088 | tf_op jit(solution)/shard_map/ppermute | solution.py:366
  95.7 4.5 %collective-permute-done.15.rb_ref = f32[3,2,128,128]{3,2,1,0:T(8,128)S(1)} collective-permute-done((f32[3,2,128,128]{3,2,1,0:T(8,128)S(1)}, f32[3,2,128,128]{3,2,1,0:T(8,128)S(1)}, u32[]{:S(2)}, u32[]{:S(2)}) %collective-permute-start.15) | collective-permute-done | bytes 393248 | tf_op jit(solution)/shard_map/ppermute | solution.py:367
  102.2 4.1 %collective-permute-start.18 = (f32[2,2,128,128]{3,2,1,0:T(8,128)S(1)}, f32[2,2,128,128]{3,2,1,0:T(8,128)S(1)}, u32[]{:S(2)}, u32[]{:S(2)}) collective-permute-start(f32[2,2,128,128]{3,2,1,0:T(8,128)S(1)} %get-tuple-element.49), channel_id=1, source_target_pairs={{1,2},{2,1},{3,4},{4,3},{5,6},{6,5},{9,10},{10,9},{11,12},{12,11},... | collective-permute-start | bytes 786440 | tf_op jit(solution)/shard_map/ppermute | solution.py:368
  106.3 5.1 %local.6.q_ref = f32[8,2,128,128]{3,2,1,0:T(8,128)S(1)} custom-call(f32[8,2,128,128]{3,2,1,0:T(8,128)S(1)} %get-tuple-element.45.w_ref, f32[8,2,128,128]{3,2,1,0:T(8,128)S(1)} %collective-permute-done.13.other_ref, f32[2048,128]{1,0:T(8,128)S(1)} %bitcast.5, bf16[1024,384]{1,0:T(8,128)(2,1)S(1)} %get-tuple-element.31.wcat_ref, ...), custom_call_target="tpu_custom_call" | custom-call | flops 2013265920 | bytes 6291456 | tf_op jit(solution)/shard_map/local/pallas_call | solution.py:251
  111.5 6.3 %collective-permute-done.17.h1_ref = f32[2,2,128,128]{3,2,1,0:T(8,128)S(1)} collective-permute-done((f32[2,2,128,128]{3,2,1,0:T(8,128)S(1)}, f32[2,2,128,128]{3,2,1,0:T(8,128)S(1)}, u32[]{:S(2)}, u32[]{:S(2)}) %collective-permute-start.17) | collective-permute-done | bytes 262176 | tf_op jit(solution)/shard_map/ppermute | solution.py:369
  117.8 5.8 %collective-permute-done.18.h2_ref = f32[2,2,128,128]{3,2,1,0:T(8,128)S(1)} collective-permute-done((f32[2,2,128,128]{3,2,1,0:T(8,128)S(1)}, f32[2,2,128,128]{3,2,1,0:T(8,128)S(1)}, u32[]{:S(2)}, u32[]{:S(2)}) %collective-permute-start.18) | collective-permute-done | bytes 262176 | tf_op jit(solution)/shard_map/ppermute | solution.py:368
  123.6 2.5 %finish.6 = (f32[8,2,128,128]{3,2,1,0:T(8,128)S(1)}, f32[5,2,128,128]{3,2,1,0:T(8,128)S(1)}, f32[3,2,128,128]{3,2,1,0:T(8,128)S(1)}, f32[2,2,128,128]{3,2,1,0:T(8,128)S(1)}, f32[2,2,128,128]{3,2,1,0:T(8,128)S(1)}) custom-call(f32[8,2,128,128]{3,2,1,0:T(8,128)S(1)} %local.6.q_ref, f32[5,2,128,128]{3,2,1,0:T(8,128)S(1)} %collective-permute-done.14.ra_ref, ...), custom_call_target="tpu_custom_call" | custom-call | flops 402653184 | bytes 4194304 | tf_op jit(solution)/shard_map/finish/pallas_call | solution.py:283
  126.2 1.9 %collective-permute-start.21 = (f32[3,2,128,128]{3,2,1,0:T(8,128)S(1)}, f32[3,2,128,128]{3,2,1,0:T(8,128)S(1)}, u32[]{:S(2)}, u32[]{:S(2)}) collective-permute-start(f32[3,2,128,128]{3,2,1,0:T(8,128)S(1)} %get-tuple-element.52), channel_id=1, source_target_pairs={{8,16},{16,8},{24,32},{32,24},{40,48},{48,40},{56,0},{64,120},{72,... | collective-permute-start | bytes 1179656 | tf_op jit(solution)/shard_map/ppermute | solution.py:367
  128.1 2.9 %collective-permute-start.20 = (f32[5,2,128,128]{3,2,1,0:T(8,128)S(1)}, f32[5,2,128,128]{3,2,1,0:T(8,128)S(1)}, u32[]{:S(2)}, u32[]{:S(2)}) collective-permute-start(f32[5,2,128,128]{3,2,1,0:T(8,128)S(1)} %get-tuple-element.51), channel_id=1, source_target_pairs={{8,16},{16,8},{24,32},{32,24},{40,48},{48,40},{56,64},{64,56},{72,... | collective-permute-start | bytes 1966088 | tf_op jit(solution)/shard_map/ppermute | solution.py:366
  131.0 5.4 %collective-permute-done.21.rb_ref = f32[3,2,128,128]{3,2,1,0:T(8,128)S(1)} collective-permute-done((f32[3,2,128,128]{3,2,1,0:T(8,128)S(1)}, f32[3,2,128,128]{3,2,1,0:T(8,128)S(1)}, u32[]{:S(2)}, u32[]{:S(2)}) %collective-permute-start.21) | collective-permute-done | bytes 393248 | tf_op jit(solution)/shard_map/ppermute | solution.py:367
  138.5 5.5 %collective-permute-start.24 = (f32[2,2,128,128]{3,2,1,0:T(8,128)S(1)}, f32[2,2,128,128]{3,2,1,0:T(8,128)S(1)}, u32[]{:S(2)}, u32[]{:S(2)}) collective-permute-start(f32[2,2,128,128]{3,2,1,0:T(8,128)S(1)} %get-tuple-element.54), channel_id=1, source_target_pairs={{1,2},{2,1},{3,4},{4,3},{5,6},{6,5},{9,10},{10,9},{11,12},{12,11},... | collective-permute-start | bytes 786440 | tf_op jit(solution)/shard_map/ppermute | solution.py:368
  144.0 5.1 %local.7.q_ref = f32[8,2,128,128]{3,2,1,0:T(8,128)S(1)} custom-call(f32[8,2,128,128]{3,2,1,0:T(8,128)S(1)} %get-tuple-element.50.w_ref, f32[8,2,128,128]{3,2,1,0:T(8,128)S(1)} %collective-permute-done.19.other_ref, f32[2048,128]{1,0:T(8,128)S(1)} %bitcast.6, bf16[1024,384]{1,0:T(8,128)(2,1)S(1)} %get-tuple-element.31.wcat_ref, ...), custom_call_target="tpu_custom_call" | custom-call | flops 2013265920 | bytes 6291456 | tf_op jit(solution)/shard_map/local/pallas_call | solution.py:251
  149.2 4.9 %collective-permute-done.23.h1_ref = f32[2,2,128,128]{3,2,1,0:T(8,128)S(1)} collective-permute-done((f32[2,2,128,128]{3,2,1,0:T(8,128)S(1)}, f32[2,2,128,128]{3,2,1,0:T(8,128)S(1)}, u32[]{:S(2)}, u32[]{:S(2)}) %collective-permute-start.23) | collective-permute-done | bytes 262176 | tf_op jit(solution)/shard_map/ppermute | solution.py:369
  154.1 5.8 %collective-permute-done.24.h2_ref = f32[2,2,128,128]{3,2,1,0:T(8,128)S(1)} collective-permute-done((f32[2,2,128,128]{3,2,1,0:T(8,128)S(1)}, f32[2,2,128,128]{3,2,1,0:T(8,128)S(1)}, u32[]{:S(2)}, u32[]{:S(2)}) %collective-permute-start.24) | collective-permute-done | bytes 262176 | tf_op jit(solution)/shard_map/ppermute | solution.py:368
  159.9 3.6 %finish.7 = f32[2048,128]{1,0:T(8,128)} custom-call(f32[8,2,128,128]{3,2,1,0:T(8,128)S(1)} %local.7.q_ref, f32[5,2,128,128]{3,2,1,0:T(8,128)S(1)} %collective-permute-done.20.ra_ref, f32[3,2,128,128]{3,2,1,0:T(8,128)S(1)} %collective-permute-done.21.rb_ref, f32[3,2,128,128]{3,2,1,0:T(8,128)S(1)} %collective-permute-done.22.rc_ref, ...), custom_call_target="tpu_custom_call" | custom-call | flops 402653184 | bytes 4194304 | tf_op jit(solution)/shard_map/finish/pallas_call | solution.py:283
  (42 shorter events, 14.6 us)
Async XLA Ops:
  0.0 1.2 copy-start
  1.2 42.5 %copy-start.1 = (f32[128,2,8,128]{3,2,1,0:T(8,128)S(1)}, f32[128,2,8,128]{3,2,1,0:T(8,128)}, u32[]{:S(2)}) copy-start(f32[128,2,8,128]{3,2,1,0:T(8,128)} %param.6) | copy-start | bytes 3145732
  2.7 41.0 %collective-permute-start = (f32[8,2,128,128]{3,2,1,0:T(8,128)}, f32[8,2,128,128]{3,2,1,0:T(8,128)}, u32[]{:S(2)}, u32[]{:S(2)}) collective-permute-start(f32[8,2,128,128]{3,2,1,0:T(8,128)} %get-tuple-element.30.w_ref), channel_id=1, source_target_pairs={{0,8},{8,0},{16,24},{24,16},{32,40},{40,32},{48,56},{56,48},{64,72... | collective-permute-start | bytes 3145736 | tf_op jit(solution)/shard_map/ppermute | solution.py:370
  2.7 10.3 %collective-permute-start.3 = (f32[3,2,128,128]{3,2,1,0:T(8,128)S(1)}, f32[3,2,128,128]{3,2,1,0:T(8,128)S(1)}, u32[]{:S(2)}, u32[]{:S(2)}) collective-permute-start(f32[3,2,128,128]{3,2,1,0:T(8,128)S(1)} %get-tuple-element.36), channel_id=1, source_target_pairs={{8,16},{16,8},{24,32},{32,24},{40,48},{48,40},{56,0},{64,120},{72,... | collective-permute-start | bytes 1179656 | tf_op jit(solution)/shard_map/ppermute | solution.py:367
  7.5 43.6 %collective-permute-start.2 = (f32[5,2,128,128]{3,2,1,0:T(8,128)}, f32[5,2,128,128]{3,2,1,0:T(8,128)S(1)}, u32[]{:S(2)}, u32[]{:S(2)}) collective-permute-start(f32[5,2,128,128]{3,2,1,0:T(8,128)} %get-tuple-element.35), channel_id=1, source_target_pairs={{8,16},{16,8},{24,32},{32,24},{40,48},{48,40},{56,64},{64,56},{72,... | collective-permute-start | bytes 1966088 | tf_op jit(solution)/shard_map/ppermute | solution.py:366
  9.4 28.8 %collective-permute-start.1 = (f32[1,2,128,128]{3,2,1,0:T(8,128)}, f32[1,2,128,128]{3,2,1,0:T(8,128)S(1)}, u32[]{:S(2)}, u32[]{:S(2)}) collective-permute-start(f32[1,2,128,128]{3,2,1,0:T(8,128)} %own_ref.1), channel_id=1, source_target_pairs={{0,8},{8,16},{16,24},{24,32},{32,40},{40,48},{48,56},{56,64},{64,7... | collective-permute-start | bytes 393224 | tf_op jit(solution)/shard_map/ppermute | solution.py:331
  13.0 38.1 %collective-permute-start.4 = (f32[3,2,128,128]{3,2,1,0:T(8,128)S(1)}, f32[3,2,128,128]{3,2,1,0:T(8,128)S(1)}, u32[]{:S(2)}, u32[]{:S(2)}) collective-permute-start(f32[3,2,128,128]{3,2,1,0:T(8,128)S(1)} %collective-permute-done.3.rb_ref), channel_id=1, source_target_pairs={{0,64},{120,56},{64,128},{184,120},{128,192},{248,184},{1,65},{121... | collective-permute-start | bytes 1179656 | tf_op jit(solution)/shard_map/ppermute | solution.py:371
  16.1 34.9 %collective-permute-start.5 = (f32[2,2,128,128]{3,2,1,0:T(8,128)}, f32[2,2,128,128]{3,2,1,0:T(8,128)S(1)}, u32[]{:S(2)}, u32[]{:S(2)}) collective-permute-start(f32[2,2,128,128]{3,2,1,0:T(8,128)} %get-tuple-element.37), channel_id=1, source_target_pairs={{0,1},{1,0},{2,3},{3,2},{4,5},{5,4},{6,7},{7,6},{8,9},{9,8},{10,11... | collective-permute-start | bytes 786440 | tf_op jit(solution)/shard_map/ppermute | solution.py:369
  38.2 2.7 %copy-start.5 = (s32[128,2]{0,1:T(2,128)S(1)}, s32[128,2]{0,1:T(2,128)}, u32[]{:S(2)}) copy-start(s32[128,2]{0,1:T(2,128)} %param.7) | copy-start | bytes 3076
  38.2 12.9 %collective-permute-start.6 = (f32[2,2,128,128]{3,2,1,0:T(8,128)S(1)}, f32[2,2,128,128]{3,2,1,0:T(8,128)S(1)}, u32[]{:S(2)}, u32[]{:S(2)}) collective-permute-start(f32[2,2,128,128]{3,2,1,0:T(8,128)S(1)} %get-tuple-element.38), channel_id=1, source_target_pairs={{1,2},{2,1},{3,4},{4,3},{5,6},{6,5},{9,10},{10,9},{11,12},{12,11},... | collective-permute-start | bytes 786440 | tf_op jit(solution)/shard_map/ppermute | solution.py:368
  40.9 0.7 copy-start.4
  41.5 1.0 copy-start.2
  42.6 0.9 copy-start.3
  53.6 17.3 %collective-permute-start.7 = (f32[8,2,128,128]{3,2,1,0:T(8,128)S(1)}, f32[8,2,128,128]{3,2,1,0:T(8,128)S(1)}, u32[]{:S(2)}, u32[]{:S(2)}) collective-permute-start(f32[8,2,128,128]{3,2,1,0:T(8,128)S(1)} %get-tuple-element.40.w_ref), channel_id=1, source_target_pairs={{0,8},{8,0},{16,24},{24,16},{32,40},{40,32},{48,56},{56,48},{64,72... | collective-permute-start | bytes 3145736 | tf_op jit(solution)/shard_map/ppermute | solution.py:370
  53.7 10.3 %collective-permute-start.9 = (f32[3,2,128,128]{3,2,1,0:T(8,128)S(1)}, f32[3,2,128,128]{3,2,1,0:T(8,128)S(1)}, u32[]{:S(2)}, u32[]{:S(2)}) collective-permute-start(f32[3,2,128,128]{3,2,1,0:T(8,128)S(1)} %get-tuple-element.42), channel_id=1, source_target_pairs={{8,16},{16,8},{24,32},{32,24},{40,48},{48,40},{56,0},{64,120},{72,... | collective-permute-start | bytes 1179656 | tf_op jit(solution)/shard_map/ppermute | solution.py:367
  55.6 31.7 %collective-permute-start.8 = (f32[5,2,128,128]{3,2,1,0:T(8,128)S(1)}, f32[5,2,128,128]{3,2,1,0:T(8,128)S(1)}, u32[]{:S(2)}, u32[]{:S(2)}) collective-permute-start(f32[5,2,128,128]{3,2,1,0:T(8,128)S(1)} %get-tuple-element.41), channel_id=1, source_target_pairs={{8,16},{16,8},{24,32},{32,24},{40,48},{48,40},{56,64},{64,56},{72,... | collective-permute-start | bytes 1966088 | tf_op jit(solution)/shard_map/ppermute | solution.py:366
  64.0 23.3 %collective-permute-start.10 = (f32[3,2,128,128]{3,2,1,0:T(8,128)S(1)}, f32[3,2,128,128]{3,2,1,0:T(8,128)S(1)}, u32[]{:S(2)}, u32[]{:S(2)}) collective-permute-start(f32[3,2,128,128]{3,2,1,0:T(8,128)S(1)} %collective-permute-done.9.rb_ref), channel_id=1, source_target_pairs={{0,64},{120,56},{64,128},{184,120},{128,192},{248,184},{1,65},{121... | collective-permute-start | bytes 1179656 | tf_op jit(solution)/shard_map/ppermute | solution.py:371
  65.9 15.7 %collective-permute-start.11 = (f32[2,2,128,128]{3,2,1,0:T(8,128)S(1)}, f32[2,2,128,128]{3,2,1,0:T(8,128)S(1)}, u32[]{:S(2)}, u32[]{:S(2)}) collective-permute-start(f32[2,2,128,128]{3,2,1,0:T(8,128)S(1)} %get-tuple-element.43), channel_id=1, source_target_pairs={{0,1},{1,0},{2,3},{3,2},{4,5},{5,4},{6,7},{7,6},{8,9},{9,8},{10,11... | collective-permute-start | bytes 786440 | tf_op jit(solution)/shard_map/ppermute | solution.py:369
  66.0 21.3 %collective-permute-start.12 = (f32[2,2,128,128]{3,2,1,0:T(8,128)S(1)}, f32[2,2,128,128]{3,2,1,0:T(8,128)S(1)}, u32[]{:S(2)}, u32[]{:S(2)}) collective-permute-start(f32[2,2,128,128]{3,2,1,0:T(8,128)S(1)} %get-tuple-element.44), channel_id=1, source_target_pairs={{1,2},{2,1},{3,4},{4,3},{5,6},{6,5},{9,10},{10,9},{11,12},{12,11},... | collective-permute-start | bytes 786440 | tf_op jit(solution)/shard_map/ppermute | solution.py:368
  89.8 16.5 %collective-permute-start.13 = (f32[8,2,128,128]{3,2,1,0:T(8,128)S(1)}, f32[8,2,128,128]{3,2,1,0:T(8,128)S(1)}, u32[]{:S(2)}, u32[]{:S(2)}) collective-permute-start(f32[8,2,128,128]{3,2,1,0:T(8,128)S(1)} %get-tuple-element.45.w_ref), channel_id=1, source_target_pairs={{0,8},{8,0},{16,24},{24,16},{32,40},{40,32},{48,56},{56,48},{64,72... | collective-permute-start | bytes 3145736 | tf_op jit(solution)/shard_map/ppermute | solution.py:370
  89.9 10.3 %collective-permute-start.15 = (f32[3,2,128,128]{3,2,1,0:T(8,128)S(1)}, f32[3,2,128,128]{3,2,1,0:T(8,128)S(1)}, u32[]{:S(2)}, u32[]{:S(2)}) collective-permute-start(f32[3,2,128,128]{3,2,1,0:T(8,128)S(1)} %get-tuple-element.47), channel_id=1, source_target_pairs={{8,16},{16,8},{24,32},{32,24},{40,48},{48,40},{56,0},{64,120},{72,... | collective-permute-start | bytes 1179656 | tf_op jit(solution)/shard_map/ppermute | solution.py:367
  91.8 31.8 %collective-permute-start.14 = (f32[5,2,128,128]{3,2,1,0:T(8,128)S(1)}, f32[5,2,128,128]{3,2,1,0:T(8,128)S(1)}, u32[]{:S(2)}, u32[]{:S(2)}) collective-permute-start(f32[5,2,128,128]{3,2,1,0:T(8,128)S(1)} %get-tuple-element.46), channel_id=1, source_target_pairs={{8,16},{16,8},{24,32},{32,24},{40,48},{48,40},{56,64},{64,56},{72,... | collective-permute-start | bytes 1966088 | tf_op jit(solution)/shard_map/ppermute | solution.py:366
  100.2 23.4 %collective-permute-start.16 = (f32[3,2,128,128]{3,2,1,0:T(8,128)S(1)}, f32[3,2,128,128]{3,2,1,0:T(8,128)S(1)}, u32[]{:S(2)}, u32[]{:S(2)}) collective-permute-start(f32[3,2,128,128]{3,2,1,0:T(8,128)S(1)} %collective-permute-done.15.rb_ref), channel_id=1, source_target_pairs={{0,64},{120,56},{64,128},{184,120},{128,192},{248,184},{1,65},{121... | collective-permute-start | bytes 1179656 | tf_op jit(solution)/shard_map/ppermute | solution.py:371
  102.1 15.7 %collective-permute-start.17 = (f32[2,2,128,128]{3,2,1,0:T(8,128)S(1)}, f32[2,2,128,128]{3,2,1,0:T(8,128)S(1)}, u32[]{:S(2)}, u32[]{:S(2)}) collective-permute-start(f32[2,2,128,128]{3,2,1,0:T(8,128)S(1)} %get-tuple-element.48), channel_id=1, source_target_pairs={{0,1},{1,0},{2,3},{3,2},{4,5},{5,4},{6,7},{7,6},{8,9},{9,8},{10,11... | collective-permute-start | bytes 786440 | tf_op jit(solution)/shard_map/ppermute | solution.py:369
  102.2 21.4 %collective-permute-start.18 = (f32[2,2,128,128]{3,2,1,0:T(8,128)S(1)}, f32[2,2,128,128]{3,2,1,0:T(8,128)S(1)}, u32[]{:S(2)}, u32[]{:S(2)}) collective-permute-start(f32[2,2,128,128]{3,2,1,0:T(8,128)S(1)} %get-tuple-element.49), channel_id=1, source_target_pairs={{1,2},{2,1},{3,4},{4,3},{5,6},{6,5},{9,10},{10,9},{11,12},{12,11},... | collective-permute-start | bytes 786440 | tf_op jit(solution)/shard_map/ppermute | solution.py:368
  126.1 18.0 %collective-permute-start.19 = (f32[8,2,128,128]{3,2,1,0:T(8,128)S(1)}, f32[8,2,128,128]{3,2,1,0:T(8,128)S(1)}, u32[]{:S(2)}, u32[]{:S(2)}) collective-permute-start(f32[8,2,128,128]{3,2,1,0:T(8,128)S(1)} %get-tuple-element.50.w_ref), channel_id=1, source_target_pairs={{0,8},{8,0},{16,24},{24,16},{32,40},{40,32},{48,56},{56,48},{64,72... | collective-permute-start | bytes 3145736 | tf_op jit(solution)/shard_map/ppermute | solution.py:370
  126.2 10.3 %collective-permute-start.21 = (f32[3,2,128,128]{3,2,1,0:T(8,128)S(1)}, f32[3,2,128,128]{3,2,1,0:T(8,128)S(1)}, u32[]{:S(2)}, u32[]{:S(2)}) collective-permute-start(f32[3,2,128,128]{3,2,1,0:T(8,128)S(1)} %get-tuple-element.52), channel_id=1, source_target_pairs={{8,16},{16,8},{24,32},{32,24},{40,48},{48,40},{56,0},{64,120},{72,... | collective-permute-start | bytes 1179656 | tf_op jit(solution)/shard_map/ppermute | solution.py:367
  128.1 31.8 %collective-permute-start.20 = (f32[5,2,128,128]{3,2,1,0:T(8,128)S(1)}, f32[5,2,128,128]{3,2,1,0:T(8,128)S(1)}, u32[]{:S(2)}, u32[]{:S(2)}) collective-permute-start(f32[5,2,128,128]{3,2,1,0:T(8,128)S(1)} %get-tuple-element.51), channel_id=1, source_target_pairs={{8,16},{16,8},{24,32},{32,24},{40,48},{48,40},{56,64},{64,56},{72,... | collective-permute-start | bytes 1966088 | tf_op jit(solution)/shard_map/ppermute | solution.py:366
  136.5 23.4 %collective-permute-start.22 = (f32[3,2,128,128]{3,2,1,0:T(8,128)S(1)}, f32[3,2,128,128]{3,2,1,0:T(8,128)S(1)}, u32[]{:S(2)}, u32[]{:S(2)}) collective-permute-start(f32[3,2,128,128]{3,2,1,0:T(8,128)S(1)} %collective-permute-done.21.rb_ref), channel_id=1, source_target_pairs={{0,64},{120,56},{64,128},{184,120},{128,192},{248,184},{1,65},{121... | collective-permute-start | bytes 1179656 | tf_op jit(solution)/shard_map/ppermute | solution.py:371
  138.4 15.7 %collective-permute-start.23 = (f32[2,2,128,128]{3,2,1,0:T(8,128)S(1)}, f32[2,2,128,128]{3,2,1,0:T(8,128)S(1)}, u32[]{:S(2)}, u32[]{:S(2)}) collective-permute-start(f32[2,2,128,128]{3,2,1,0:T(8,128)S(1)} %get-tuple-element.53), channel_id=1, source_target_pairs={{0,1},{1,0},{2,3},{3,2},{4,5},{5,4},{6,7},{7,6},{8,9},{9,8},{10,11... | collective-permute-start | bytes 786440 | tf_op jit(solution)/shard_map/ppermute | solution.py:369
  138.5 21.4 %collective-permute-start.24 = (f32[2,2,128,128]{3,2,1,0:T(8,128)S(1)}, f32[2,2,128,128]{3,2,1,0:T(8,128)S(1)}, u32[]{:S(2)}, u32[]{:S(2)}) collective-permute-start(f32[2,2,128,128]{3,2,1,0:T(8,128)S(1)} %get-tuple-element.54), channel_id=1, source_target_pairs={{1,2},{2,1},{3,4},{4,3},{5,6},{6,5},{9,10},{10,9},{11,12},{12,11},... | collective-permute-start | bytes 786440 | tf_op jit(solution)/shard_map/ppermute | solution.py:368

commit v2 on v1

--- a/solution.py
+++ b/solution.py
@@ -37,8 +37,7 @@
     return pl.BlockSpec(shape, lambda *_: zeros)
 
 
-def row_spec():
-    return pl.BlockSpec((1, 2, 128, 128), lambda i: (i, 0, 0, 0))
+VMEM = pl.BlockSpec(memory_space=pltpu.VMEM)
 
 
 SCALAR = pl.BlockSpec(memory_space=pltpu.SMEM)
@@ -50,7 +49,7 @@
 
 
 def row_radius(i):
-    row = lax.axis_index("tile") * 8 + i
+    row = lax.axis_index("tile") * 8 + jnp.int32(i)
     return radius_start + grid_step * row.astype(F32)
 
 
@@ -140,100 +139,90 @@
 
 
 def local_kernel(step, w_ref, other_ref, psi_ref, wcat_ref, d_ref, radial_ref, ang_ref, q_ref):
-    i = pl.program_id(0)
-    mine = both(w_ref, i)
-    prod = jnp.dot(wcat_ref[...], operand(mine), preferred_element_type=F32)
-    total = dipole_part(i, d_ref, both(other_ref, 0))
-    for k in range(NMP):
-        total = total + radial_ref[k, pl.ds(i, 1), :] * prod[k * 128 : (k + 1) * 128]
-    for shift in (-2, -1, 1, 2):
-        place = i + shift
-        inside = jnp.logical_and(place >= 0, place < 8)
-        weight = jnp.where(inside, NEAR if abs(shift) == 1 else FAR, 0.0)
-        place = jnp.clip(place, 0, 7)
-        total = total + weight * both(w_ref, place)
-    one = row_radius(i)
-    two = col_radius((1, 128))
-    lane = lax.broadcasted_iota(jnp.int32, (1, 128), 1)
-    potential = (
-        ang_ref[0] * (1.0 / (one * one))
-        + ang_ref[1] * (1.0 / (two * two))
-        + (CENTRE - 2.0 / one - 2.0 / two)
-    )
-    half = []
-    for part in range(2):
-        value = mine[:, part * 128 : (part + 1) * 128]
-        near = jnp.where(lane >= 1, pltpu.roll(value, 1, 1), 0.0) + jnp.where(
-            lane < 127, pltpu.roll(value, 127, 1), 0.0
+    def row(i, carry):
+        mine = both(w_ref, i)
+        prod = jnp.dot(wcat_ref[...], operand(mine), preferred_element_type=F32)
+        total = dipole_part(i, d_ref, both(other_ref, i))
+        for k in range(NMP):
+            total = total + radial_ref[k, pl.ds(i, 1), :] * prod[k * 128 : (k + 1) * 128]
+        for shift in (-2, -1, 1, 2):
+            place = i + shift
+            inside = jnp.logical_and(place >= 0, place < 8)
+            weight = jnp.where(inside, NEAR if abs(shift) == 1 else FAR, 0.0)
+            place = jnp.clip(place, 0, 7)
+            total = total + weight * both(w_ref, place)
+        one = row_radius(i)
+        two = col_radius((1, 128))
+        lane = lax.broadcasted_iota(jnp.int32, (1, 128), 1)
+        potential = (
+            ang_ref[0] * (1.0 / (one * one))
+            + ang_ref[1] * (1.0 / (two * two))
+            + (CENTRE - 2.0 / one - 2.0 / two)
         )
-        far = jnp.where(lane >= 2, pltpu.roll(value, 2, 1), 0.0) + jnp.where(
-            lane < 126, pltpu.roll(value, 126, 1), 0.0
-        )
-        half.append(
-            total[:, part * 128 : (part + 1) * 128] + potential * value + NEAR * near + FAR * far
-        )
-    q_ref[0, 0] = natural(psi_ref, i, 0) + step * half[1]
-    q_ref[0, 1] = natural(psi_ref, i, 1) - step * half[0]
-
-
-def far_row(i, ra_ref, rb_ref, rc_ref):
+        half = []
+        for part in range(2):
+            value = mine[:, part * 128 : (part + 1) * 128]
+            near = jnp.where(lane >= 1, pltpu.roll(value, 1, 1), 0.0) + jnp.where(
+                lane < 127, pltpu.roll(value, 127, 1), 0.0
+            )
+            far = jnp.where(lane >= 2, pltpu.roll(value, 2, 1), 0.0) + jnp.where(
+                lane < 126, pltpu.roll(value, 126, 1), 0.0
+            )
+            half.append(
+                total[:, part * 128 : (part + 1) * 128]
+                + potential * value
+                + NEAR * near
+                + FAR * far
+            )
+        q_ref[i, 0] = natural(psi_ref, i, 0) + step * half[1]
+        q_ref[i, 1] = natural(psi_ref, i, 1) - step * half[0]
+        return carry
+
+    lax.fori_loop(0, 8, row, 0)
+
+
+def finish_kernel(last, step, q_ref, ra_ref, rb_ref, rc_ref, h1_ref, h2_ref, d_ref, *refs):
     place = lax.rem(lax.axis_index("lblk"), 8)
     relayed = jnp.logical_or(place == 0, place == 7)
-    parts = [
-        jnp.where(
-            i < STRAIGHT, ra_ref[0, part], jnp.where(relayed, rc_ref[0, part], rb_ref[0, part])
-        )
-        for part in range(2)
-    ]
-    return jnp.concatenate(parts, axis=1)
-
-
-def finish_kernel(last, step, q_ref, ra_ref, rb_ref, rc_ref, h1_ref, h2_ref, d_ref, *refs):
-    if last:
-        out_ref, g_ref = refs
-    else:
-        out_ref, fa_ref, fb_ref, s1_ref, s2_ref, g_ref = refs
-    i = pl.program_id(0)
     even = lax.rem(lax.axis_index("tile"), 2) == 0
-    g_ref[...] = dipole_part(i, d_ref, far_row(i, ra_ref, rb_ref, rc_ref))
-    low = i < 2
-    high = i >= 6
-    zero = jnp.float32(0.0)
-    c0 = jnp.where(low, jnp.where(i == 0, FAR, zero), jnp.where(i == 6, FAR, NEAR))
-    c1 = jnp.where(low, jnp.where(i == 0, NEAR, FAR), jnp.where(i == 6, zero, FAR))
-    use1 = jnp.logical_or(jnp.logical_and(low, ~even), jnp.logical_and(high, even))
-    use2 = jnp.logical_or(jnp.logical_and(low, even), jnp.logical_and(high, ~even))
-
-    def halo(ref):
-        for part in range(2):
-            cols = pl.ds(part * 128, 128)
-            g_ref[:, cols] += c0 * ref[0, part] + c1 * ref[1, part]
-
-    @pl.when(use1)
-    def _():
-        halo(h1_ref)
-
-    @pl.when(use2)
-    def _():
-        halo(h2_ref)
-
-    real = q_ref[0, 0] + step * g_ref[:, 128:]
-    imag = q_ref[0, 1] - step * g_ref[:, :128]
-    if last:
-        out_ref[pl.ds(i, 128, stride=16), :] = real
-        out_ref[pl.ds(8 + i, 128, stride=16), :] = imag
-        return
-
-    def store(ref, row):
-        ref[row, 0] = real
-        ref[row, 1] = imag
-
-    slot = jnp.where(low, i, i - 6)
-    store(out_ref, 0)
-    pl.when(i < STRAIGHT)(lambda: store(fa_ref, 0))
-    pl.when(i >= STRAIGHT)(lambda: store(fb_ref, 0))
-    pl.when(use1)(lambda: store(s1_ref, slot))
-    pl.when(use2)(lambda: store(s2_ref, slot))
+    for i in range(8):
+        if i < STRAIGHT:
+            other = both(ra_ref, i)
+        else:
+            late = i - STRAIGHT
+            other = jnp.where(relayed, both(rc_ref, late), both(rb_ref, late))
+        total = dipole_part(i, d_ref, other)
+        if i < 2 or i >= 6:
+            weights = {0: (FAR, NEAR), 1: (None, FAR), 6: (FAR, None), 7: (NEAR, FAR)}[i]
+            for row, weight in enumerate(weights):
+                if weight is not None:
+                    one, two = both(h1_ref, row), both(h2_ref, row)
+                    total = total + weight * (
+                        jnp.where(even, two, one) if i < 2 else jnp.where(even, one, two)
+                    )
+        real = q_ref[i, 0] + step * total[:, 128:]
+        imag = q_ref[i, 1] - step * total[:, :128]
+        if last:
+            refs[0][pl.ds(i, 128, stride=16), :] = real
+            refs[0][pl.ds(8 + i, 128, stride=16), :] = imag
+            continue
+        w_ref, fa_ref, fb_ref, s1_ref, s2_ref = refs
+
+        def store(ref, row):
+            ref[row, 0] = real
+            ref[row, 1] = imag
+
+        store(w_ref, i)
+        if i < STRAIGHT:
+            store(fa_ref, i)
+        else:
+            store(fb_ref, i - STRAIGHT)
+        if i < 2:
+            pl.when(even)(functools.partial(store, s2_ref, i))
+            pl.when(jnp.logical_not(even))(functools.partial(store, s1_ref, i))
+        if i >= 6:
+            pl.when(even)(functools.partial(store, s1_ref, i - 6))
+            pl.when(jnp.logical_not(even))(functools.partial(store, s2_ref, i - 6))
 
 
 FIELD = (8, 2, 128, 128)
@@ -247,60 +236,39 @@
     return jax.ShapeDtypeStruct(dims, dtype)
 
 
-def local_call(step, w, other, psi, wcat, d, radial, ang):
+def call(kernel, inputs, outputs, flops, moved, limit=40 << 20):
     return pl.pallas_call(
+        kernel,
+        in_specs=[SCALAR if small else VMEM for _, small in inputs],
+        out_specs=[VMEM] * len(outputs),
+        out_shape=[shape(*o) if isinstance(o[0], tuple) else shape(o) for o in outputs],
+        compiler_params=params(limit),
+        cost_estimate=cost(flops, moved),
+    )(*[value for value, _ in inputs])
+
+
+def local_call(step, *operands):
+    (q,) = call(
         functools.partial(local_kernel, step),
-        grid=(8,),
-        in_specs=[
-            whole(FIELD),
-            row_spec(),
-            whole(FLAT),
-            whole((1024, 384)),
-            whole((256, 384)),
-            whole((8, 8, 256)),
-            whole((2, 128, 128)),
-        ],
-        out_specs=row_spec(),
-        out_shape=shape(FIELD),
-        compiler_params=params(),
-        cost_estimate=cost(2 * 2048 * 1280 * 384, 6 << 20),
-        name="local",
-    )(w, other, psi, wcat, d, radial, ang)
-
-
-def early_rows():
-    return pl.BlockSpec((1, 2, 128, 128), lambda i: (jnp.minimum(i, STRAIGHT - 1), 0, 0, 0))
-
-
-def late_rows():
-    return pl.BlockSpec((1, 2, 128, 128), lambda i: (jnp.maximum(i - STRAIGHT, 0), 0, 0, 0))
+        [(value, False) for value in operands],
+        [FIELD],
+        2 * 2048 * 1280 * 384,
+        6 << 20,
+    )
+    return q
 
 
 SENT = [FIELD, EARLY, LATE, EDGE, EDGE]
 
 
-def finish_call(last, step, q, ra, rb, rc, h1, h2, d):
-    return pl.pallas_call(
+def finish_call(last, step, *operands):
+    return call(
         functools.partial(finish_kernel, last, step),
-        grid=(8,),
-        in_specs=[
-            row_spec(),
-            early_rows(),
-            late_rows(),
-            late_rows(),
-            whole(EDGE),
-            whole(EDGE),
-            whole((256, 384)),
-        ],
-        out_specs=[whole(FLAT)]
-        if last
-        else [row_spec(), early_rows(), late_rows(), whole(EDGE), whole(EDGE)],
-        out_shape=[shape(dims) for dims in ([FLAT] if last else SENT)],
-        scratch_shapes=[pltpu.VMEM((128, 256), F32)],
-        compiler_params=params(),
-        cost_estimate=cost(2 * 2048 * 256 * 384, 4 << 20),
-        name="finish",
-    )(q, ra, rb, rc, h1, h2, d)
+        [(value, False) for value in operands],
+        [FLAT] if last else SENT,
+        2 * 2048 * 256 * 384,
+        4 << 20,
+    )
 
 
 def swaps(count, start):

time: 165 us -> 160 us (0.970)
  Pallas kernels: 36.2 us -> 30.6 us
    pallas_call x8, Pallas kernels: 33.7 us -> 28.1 us  [call(): pl.pallas_call(kernel, in_specs=[SCALAR if small else VMEM for _, small i...]
  transfers between devices with their start and end apart: 25 -> 25, of which waited for: 11 -> 11; matrix products, arithmetic and copies ran while one was open for 0% -> 0% of each run, Pallas kernels for 15% -> 14%
where the time goes in v2:
time: 160 us; the launch traced here: 158 us
  waiting for transfers between devices  73.5 us (46%)
  starting transfers between devices  50.1 us (31%)
  Pallas kernels  30.6 us (19%)
  local copies, waits for them, and re-layouts  3.03 us (2%)
    pallas_call x8, Pallas kernels, call(): pl.pallas_call(kernel, in_specs=[SCALAR if small else VMEM for _, small i...  28.1 us
    ppermute x1, waiting for transfers between devices, per_device(): lax.ppermute(dipole, 'lblk', [(k, k + 1) for k in range(blocks - 1)])  20.9 us
    ppermute x4, waiting for transfers between devices, per_device(): rb = lax.ppermute(fb, 'lblk', relay)  18.1 us
    ppermute x4, waiting for transfers between devices, per_device(): h2 = lax.ppermute(s2, 'tile', swaps(tiles, 1))  17.4 us
    ppermute x4, waiting for transfers between devices, per_device(): h1 = lax.ppermute(s1, 'tile', swaps(tiles, 0))  17.1 us
    ppermute x4, starting transfers between devices, per_device(): h2 = lax.ppermute(s2, 'tile', swaps(tiles, 1))  16.5 us
    ppermute x4, starting transfers between devices, per_device(): ra = lax.ppermute(fa, 'lblk', swaps(blocks, 1))  10.6 us
    ppermute x4, starting transfers between devices, per_device(): rb = lax.ppermute(fb, 'lblk', relay)  10.5 us
  transfers between devices with their start and end apart: 25, of which 11 were waited for; matrix products, arithmetic and copies ran while one was open for 0% of the time, Pallas kernels for 14%

profile of v2, /device:TPU:152, one launch (start us, length us, event | category | flops | bytes accessed | tf_op | source)
XLA Modules:
  0.0 158.2 jit_solution(14943030395695502854)
XLA Ops:
  2.7 4.8 %collective-permute-start.3 = (f32[3,2,128,128]{3,2,1,0:T(8,128)S(1)}, f32[3,2,128,128]{3,2,1,0:T(8,128)S(1)}, u32[]{:S(2)}, u32[]{:S(2)}) collective-permute-start(f32[3,2,128,128]{3,2,1,0:T(8,128)S(1)} %get-tuple-element.36), channel_id=1, source_target_pairs={{8,16},{16,8},{24,32},{32,24},{40,48},{48,40},{56,0},{64,120},{72,... | collective-permute-start | bytes 1179656 | tf_op jit(solution)/shard_map/ppermute | solution.py:335
  7.5 1.9 %collective-permute-start.2 = (f32[5,2,128,128]{3,2,1,0:T(8,128)}, f32[5,2,128,128]{3,2,1,0:T(8,128)S(1)}, u32[]{:S(2)}, u32[]{:S(2)}) collective-permute-start(f32[5,2,128,128]{3,2,1,0:T(8,128)} %get-tuple-element.35), channel_id=1, source_target_pairs={{8,16},{16,8},{24,32},{32,24},{40,48},{48,40},{56,64},{64,56},{72,... | collective-permute-start | bytes 1966088 | tf_op jit(solution)/shard_map/ppermute | solution.py:334
  9.4 1.9 %collective-permute-start.1 = (f32[1,2,128,128]{3,2,1,0:T(8,128)}, f32[1,2,128,128]{3,2,1,0:T(8,128)S(1)}, u32[]{:S(2)}, u32[]{:S(2)}) collective-permute-start(f32[1,2,128,128]{3,2,1,0:T(8,128)} %own_ref.1), channel_id=1, source_target_pairs={{0,8},{8,16},{16,24},{24,32},{32,40},{40,48},{48,56},{56,64},{64,7... | collective-permute-start | bytes 393224 | tf_op jit(solution)/shard_map/ppermute | solution.py:299
  13.0 3.1 %collective-permute-start.4 = (f32[3,2,128,128]{3,2,1,0:T(8,128)S(1)}, f32[3,2,128,128]{3,2,1,0:T(8,128)S(1)}, u32[]{:S(2)}, u32[]{:S(2)}) collective-permute-start(f32[3,2,128,128]{3,2,1,0:T(8,128)S(1)} %collective-permute-done.3.rb_ref), channel_id=1, source_target_pairs={{0,64},{120,56},{64,128},{184,120},{128,192},{248,184},{1,65},{121... | collective-permute-start | bytes 1179656 | tf_op jit(solution)/shard_map/ppermute | solution.py:339
  17.2 20.9 %collective-permute-done.1.below_ref = f32[1,2,128,128]{3,2,1,0:T(8,128)S(1)} collective-permute-done((f32[1,2,128,128]{3,2,1,0:T(8,128)}, f32[1,2,128,128]{3,2,1,0:T(8,128)S(1)}, u32[]{:S(2)}, u32[]{:S(2)}) %collective-permute-start.1) | collective-permute-done | bytes 131104 | tf_op jit(solution)/shard_map/ppermute | solution.py:299
  38.2 2.0 %collective-permute-start.6 = (f32[2,2,128,128]{3,2,1,0:T(8,128)S(1)}, f32[2,2,128,128]{3,2,1,0:T(8,128)S(1)}, u32[]{:S(2)}, u32[]{:S(2)}) collective-permute-start(f32[2,2,128,128]{3,2,1,0:T(8,128)S(1)} %get-tuple-element.38), channel_id=1, source_target_pairs={{1,2},{2,1},{3,4},{4,3},{5,6},{6,5},{9,10},{10,9},{11,12},{12,11},... | collective-permute-start | bytes 786440 | tf_op jit(solution)/shard_map/ppermute | solution.py:336
  43.7 6.6 %shard_map.64.q_ref = f32[8,2,128,128]{3,2,1,0:T(8,128)S(1)} custom-call(f32[8,2,128,128]{3,2,1,0:T(8,128)} %get-tuple-element.30.w_ref, f32[8,2,128,128]{3,2,1,0:T(8,128)} %collective-permute-done.other_ref, f32[2048,128]{1,0:T(8,128)S(1)} %bitcast.3, bf16[1024,384]{1,0:T(8,128)(2,1)S(1)} %get-tuple-element.31.wcat_ref, ...), custom_call_target="tpu_custom_call" | custom-call | flops 2013265920 | bytes 6291456 | tf_op jit(solution)/shard_map/pallas_call | solution.py:240
  52.0 1.9 %collective-permute-start.9 = (f32[3,2,128,128]{3,2,1,0:T(8,128)S(1)}, f32[3,2,128,128]{3,2,1,0:T(8,128)S(1)}, u32[]{:S(2)}, u32[]{:S(2)}) collective-permute-start(f32[3,2,128,128]{3,2,1,0:T(8,128)S(1)} %get-tuple-element.42), channel_id=1, source_target_pairs={{8,16},{16,8},{24,32},{32,24},{40,48},{48,40},{56,0},{64,120},{72,... | collective-permute-start | bytes 1179656 | tf_op jit(solution)/shard_map/ppermute | solution.py:335
  53.9 1.9 %collective-permute-start.8 = (f32[5,2,128,128]{3,2,1,0:T(8,128)S(1)}, f32[5,2,128,128]{3,2,1,0:T(8,128)S(1)}, u32[]{:S(2)}, u32[]{:S(2)}) collective-permute-start(f32[5,2,128,128]{3,2,1,0:T(8,128)S(1)} %get-tuple-element.41), channel_id=1, source_target_pairs={{8,16},{16,8},{24,32},{32,24},{40,48},{48,40},{56,64},{64,56},{72,... | collective-permute-start | bytes 1966088 | tf_op jit(solution)/shard_map/ppermute | solution.py:334
  55.9 6.4 %collective-permute-done.9.rb_ref = f32[3,2,128,128]{3,2,1,0:T(8,128)S(1)} collective-permute-done((f32[3,2,128,128]{3,2,1,0:T(8,128)S(1)}, f32[3,2,128,128]{3,2,1,0:T(8,128)S(1)}, u32[]{:S(2)}, u32[]{:S(2)}) %collective-permute-start.9) | collective-permute-done | bytes 393248 | tf_op jit(solution)/shard_map/ppermute | solution.py:335
  62.3 1.9 %collective-permute-start.10 = (f32[3,2,128,128]{3,2,1,0:T(8,128)S(1)}, f32[3,2,128,128]{3,2,1,0:T(8,128)S(1)}, u32[]{:S(2)}, u32[]{:S(2)}) collective-permute-start(f32[3,2,128,128]{3,2,1,0:T(8,128)S(1)} %collective-permute-done.9.rb_ref), channel_id=1, source_target_pairs={{0,64},{120,56},{64,128},{184,120},{128,192},{248,184},{1,65},{121... | collective-permute-start | bytes 1179656 | tf_op jit(solution)/shard_map/ppermute | solution.py:339
  64.3 4.9 %collective-permute-start.12 = (f32[2,2,128,128]{3,2,1,0:T(8,128)S(1)}, f32[2,2,128,128]{3,2,1,0:T(8,128)S(1)}, u32[]{:S(2)}, u32[]{:S(2)}) collective-permute-start(f32[2,2,128,128]{3,2,1,0:T(8,128)S(1)} %get-tuple-element.44), channel_id=1, source_target_pairs={{1,2},{2,1},{3,4},{4,3},{5,6},{6,5},{9,10},{10,9},{11,12},{12,11},... | collective-permute-start | bytes 786440 | tf_op jit(solution)/shard_map/ppermute | solution.py:336
  69.2 5.0 %shard_map.66.q_ref = f32[8,2,128,128]{3,2,1,0:T(8,128)S(1)} custom-call(f32[8,2,128,128]{3,2,1,0:T(8,128)S(1)} %get-tuple-element.40.w_ref, f32[8,2,128,128]{3,2,1,0:T(8,128)S(1)} %collective-permute-done.7.other_ref, f32[2048,128]{1,0:T(8,128)S(1)} %bitcast.4, bf16[1024,384]{1,0:T(8,128)(2,1)S(1)} %get-tuple-element.31.wcat_ref, ...), custom_call_target="tpu_custom_call" | custom-call | flops 2013265920 | bytes 6291456 | tf_op jit(solution)/shard_map/pallas_call | solution.py:240
  74.2 5.7 %collective-permute-done.11.h1_ref = f32[2,2,128,128]{3,2,1,0:T(8,128)S(1)} collective-permute-done((f32[2,2,128,128]{3,2,1,0:T(8,128)S(1)}, f32[2,2,128,128]{3,2,1,0:T(8,128)S(1)}, u32[]{:S(2)}, u32[]{:S(2)}) %collective-permute-start.11) | collective-permute-done | bytes 262176 | tf_op jit(solution)/shard_map/ppermute | solution.py:337
  79.9 5.8 %collective-permute-done.12.h2_ref = f32[2,2,128,128]{3,2,1,0:T(8,128)S(1)} collective-permute-done((f32[2,2,128,128]{3,2,1,0:T(8,128)S(1)}, f32[2,2,128,128]{3,2,1,0:T(8,128)S(1)}, u32[]{:S(2)}, u32[]{:S(2)}) %collective-permute-start.12) | collective-permute-done | bytes 262176 | tf_op jit(solution)/shard_map/ppermute | solution.py:336
  87.3 1.9 %collective-permute-start.15 = (f32[3,2,128,128]{3,2,1,0:T(8,128)S(1)}, f32[3,2,128,128]{3,2,1,0:T(8,128)S(1)}, u32[]{:S(2)}, u32[]{:S(2)}) collective-permute-start(f32[3,2,128,128]{3,2,1,0:T(8,128)S(1)} %get-tuple-element.47), channel_id=1, source_target_pairs={{8,16},{16,8},{24,32},{32,24},{40,48},{48,40},{56,0},{64,120},{72,... | collective-permute-start | bytes 1179656 | tf_op jit(solution)/shard_map/ppermute | solution.py:335
  89.2 3.9 %collective-permute-start.14 = (f32[5,2,128,128]{3,2,1,0:T(8,128)S(1)}, f32[5,2,128,128]{3,2,1,0:T(8,128)S(1)}, u32[]{:S(2)}, u32[]{:S(2)}) collective-permute-start(f32[5,2,128,128]{3,2,1,0:T(8,128)S(1)} %get-tuple-element.46), channel_id=1, source_target_pairs={{8,16},{16,8},{24,32},{32,24},{40,48},{48,40},{56,64},{64,56},{72,... | collective-permute-start | bytes 1966088 | tf_op jit(solution)/shard_map/ppermute | solution.py:334
  93.1 4.5 %collective-permute-done.15.rb_ref = f32[3,2,128,128]{3,2,1,0:T(8,128)S(1)} collective-permute-done((f32[3,2,128,128]{3,2,1,0:T(8,128)S(1)}, f32[3,2,128,128]{3,2,1,0:T(8,128)S(1)}, u32[]{:S(2)}, u32[]{:S(2)}) %collective-permute-start.15) | collective-permute-done | bytes 393248 | tf_op jit(solution)/shard_map/ppermute | solution.py:335
  97.6 1.9 %collective-permute-start.16 = (f32[3,2,128,128]{3,2,1,0:T(8,128)S(1)}, f32[3,2,128,128]{3,2,1,0:T(8,128)S(1)}, u32[]{:S(2)}, u32[]{:S(2)}) collective-permute-start(f32[3,2,128,128]{3,2,1,0:T(8,128)S(1)} %collective-permute-done.15.rb_ref), channel_id=1, source_target_pairs={{0,64},{120,56},{64,128},{184,120},{128,192},{248,184},{1,65},{121... | collective-permute-start | bytes 1179656 | tf_op jit(solution)/shard_map/ppermute | solution.py:339
  99.6 4.1 %collective-permute-start.18 = (f32[2,2,128,128]{3,2,1,0:T(8,128)S(1)}, f32[2,2,128,128]{3,2,1,0:T(8,128)S(1)}, u32[]{:S(2)}, u32[]{:S(2)}) collective-permute-start(f32[2,2,128,128]{3,2,1,0:T(8,128)S(1)} %get-tuple-element.49), channel_id=1, source_target_pairs={{1,2},{2,1},{3,4},{4,3},{5,6},{6,5},{9,10},{10,9},{11,12},{12,11},... | collective-permute-start | bytes 786440 | tf_op jit(solution)/shard_map/ppermute | solution.py:336
  103.7 5.0 %shard_map.68.q_ref = f32[8,2,128,128]{3,2,1,0:T(8,128)S(1)} custom-call(f32[8,2,128,128]{3,2,1,0:T(8,128)S(1)} %get-tuple-element.45.w_ref, f32[8,2,128,128]{3,2,1,0:T(8,128)S(1)} %collective-permute-done.13.other_ref, f32[2048,128]{1,0:T(8,128)S(1)} %bitcast.5, bf16[1024,384]{1,0:T(8,128)(2,1)S(1)} %get-tuple-element.31.wcat_ref, ...), custom_call_target="tpu_custom_call" | custom-call | flops 2013265920 | bytes 6291456 | tf_op jit(solution)/shard_map/pallas_call | solution.py:240
  108.7 6.4 %collective-permute-done.17.h1_ref = f32[2,2,128,128]{3,2,1,0:T(8,128)S(1)} collective-permute-done((f32[2,2,128,128]{3,2,1,0:T(8,128)S(1)}, f32[2,2,128,128]{3,2,1,0:T(8,128)S(1)}, u32[]{:S(2)}, u32[]{:S(2)}) %collective-permute-start.17) | collective-permute-done | bytes 262176 | tf_op jit(solution)/shard_map/ppermute | solution.py:337
  115.2 5.8 %collective-permute-done.18.h2_ref = f32[2,2,128,128]{3,2,1,0:T(8,128)S(1)} collective-permute-done((f32[2,2,128,128]{3,2,1,0:T(8,128)S(1)}, f32[2,2,128,128]{3,2,1,0:T(8,128)S(1)}, u32[]{:S(2)}, u32[]{:S(2)}) %collective-permute-start.18) | collective-permute-done | bytes 262176 | tf_op jit(solution)/shard_map/ppermute | solution.py:336
  122.5 1.9 %collective-permute-start.21 = (f32[3,2,128,128]{3,2,1,0:T(8,128)S(1)}, f32[3,2,128,128]{3,2,1,0:T(8,128)S(1)}, u32[]{:S(2)}, u32[]{:S(2)}) collective-permute-start(f32[3,2,128,128]{3,2,1,0:T(8,128)S(1)} %get-tuple-element.52), channel_id=1, source_target_pairs={{8,16},{16,8},{24,32},{32,24},{40,48},{48,40},{56,0},{64,120},{72,... | collective-permute-start | bytes 1179656 | tf_op jit(solution)/shard_map/ppermute | solution.py:335
  124.5 2.9 %collective-permute-start.20 = (f32[5,2,128,128]{3,2,1,0:T(8,128)S(1)}, f32[5,2,128,128]{3,2,1,0:T(8,128)S(1)}, u32[]{:S(2)}, u32[]{:S(2)}) collective-permute-start(f32[5,2,128,128]{3,2,1,0:T(8,128)S(1)} %get-tuple-element.51), channel_id=1, source_target_pairs={{8,16},{16,8},{24,32},{32,24},{40,48},{48,40},{56,64},{64,56},{72,... | collective-permute-start | bytes 1966088 | tf_op jit(solution)/shard_map/ppermute | solution.py:334
  127.4 5.4 %collective-permute-done.21.rb_ref = f32[3,2,128,128]{3,2,1,0:T(8,128)S(1)} collective-permute-done((f32[3,2,128,128]{3,2,1,0:T(8,128)S(1)}, f32[3,2,128,128]{3,2,1,0:T(8,128)S(1)}, u32[]{:S(2)}, u32[]{:S(2)}) %collective-permute-start.21) | collective-permute-done | bytes 393248 | tf_op jit(solution)/shard_map/ppermute | solution.py:335
  132.9 1.9 %collective-permute-start.22 = (f32[3,2,128,128]{3,2,1,0:T(8,128)S(1)}, f32[3,2,128,128]{3,2,1,0:T(8,128)S(1)}, u32[]{:S(2)}, u32[]{:S(2)}) collective-permute-start(f32[3,2,128,128]{3,2,1,0:T(8,128)S(1)} %collective-permute-done.21.rb_ref), channel_id=1, source_target_pairs={{0,64},{120,56},{64,128},{184,120},{128,192},{248,184},{1,65},{121... | collective-permute-start | bytes 1179656 | tf_op jit(solution)/shard_map/ppermute | solution.py:339
  134.9 5.5 %collective-permute-start.24 = (f32[2,2,128,128]{3,2,1,0:T(8,128)S(1)}, f32[2,2,128,128]{3,2,1,0:T(8,128)S(1)}, u32[]{:S(2)}, u32[]{:S(2)}) collective-permute-start(f32[2,2,128,128]{3,2,1,0:T(8,128)S(1)} %get-tuple-element.54), channel_id=1, source_target_pairs={{1,2},{2,1},{3,4},{4,3},{5,6},{6,5},{9,10},{10,9},{11,12},{12,11},... | collective-permute-start | bytes 786440 | tf_op jit(solution)/shard_map/ppermute | solution.py:336
  140.4 5.0 %shard_map.70.q_ref = f32[8,2,128,128]{3,2,1,0:T(8,128)S(1)} custom-call(f32[8,2,128,128]{3,2,1,0:T(8,128)S(1)} %get-tuple-element.50.w_ref, f32[8,2,128,128]{3,2,1,0:T(8,128)S(1)} %collective-permute-done.19.other_ref, f32[2048,128]{1,0:T(8,128)S(1)} %bitcast.6, bf16[1024,384]{1,0:T(8,128)(2,1)S(1)} %get-tuple-element.31.wcat_ref, ...), custom_call_target="tpu_custom_call" | custom-call | flops 2013265920 | bytes 6291456 | tf_op jit(solution)/shard_map/pallas_call | solution.py:240
  145.4 5.0 %collective-permute-done.23.h1_ref = f32[2,2,128,128]{3,2,1,0:T(8,128)S(1)} collective-permute-done((f32[2,2,128,128]{3,2,1,0:T(8,128)S(1)}, f32[2,2,128,128]{3,2,1,0:T(8,128)S(1)}, u32[]{:S(2)}, u32[]{:S(2)}) %collective-permute-start.23) | collective-permute-done | bytes 262176 | tf_op jit(solution)/shard_map/ppermute | solution.py:337
  150.4 5.8 %collective-permute-done.24.h2_ref = f32[2,2,128,128]{3,2,1,0:T(8,128)S(1)} collective-permute-done((f32[2,2,128,128]{3,2,1,0:T(8,128)S(1)}, f32[2,2,128,128]{3,2,1,0:T(8,128)S(1)}, u32[]{:S(2)}, u32[]{:S(2)}) %collective-permute-start.24) | collective-permute-done | bytes 262176 | tf_op jit(solution)/shard_map/ppermute | solution.py:336
  156.3 1.9 %shard_map.71 = f32[2048,128]{1,0:T(8,128)} custom-call(f32[8,2,128,128]{3,2,1,0:T(8,128)S(1)} %shard_map.70.q_ref, f32[5,2,128,128]{3,2,1,0:T(8,128)S(1)} %collective-permute-done.20.ra_ref, f32[3,2,128,128]{3,2,1,0:T(8,128)S(1)} %collective-permute-done.21.rb_ref, f32[3,2,128,128]{3,2,1,0:T(8,128)S(1)} %collective-permute-done.22.rc_ref, ...), custom_call_target="tpu_custom_call" | custom-call | flops 402653184 | bytes 4194304 | tf_op jit(solution)/shard_map/pallas_call | solution.py:240
  (42 shorter events, 13.3 us)
Async XLA Ops:
  0.0 1.2 copy-start
  1.2 42.5 %copy-start.1 = (f32[128,2,8,128]{3,2,1,0:T(8,128)S(1)}, f32[128,2,8,128]{3,2,1,0:T(8,128)}, u32[]{:S(2)}) copy-start(f32[128,2,8,128]{3,2,1,0:T(8,128)} %param.6) | copy-start | bytes 3145732
  2.7 41.0 %collective-permute-start = (f32[8,2,128,128]{3,2,1,0:T(8,128)}, f32[8,2,128,128]{3,2,1,0:T(8,128)}, u32[]{:S(2)}, u32[]{:S(2)}) collective-permute-start(f32[8,2,128,128]{3,2,1,0:T(8,128)} %get-tuple-element.30.w_ref), channel_id=1, source_target_pairs={{0,8},{8,0},{16,24},{24,16},{32,40},{40,32},{48,56},{56,48},{64,72... | collective-permute-start | bytes 3145736 | tf_op jit(solution)/shard_map/ppermute | solution.py:338
  2.7 10.3 %collective-permute-start.3 = (f32[3,2,128,128]{3,2,1,0:T(8,128)S(1)}, f32[3,2,128,128]{3,2,1,0:T(8,128)S(1)}, u32[]{:S(2)}, u32[]{:S(2)}) collective-permute-start(f32[3,2,128,128]{3,2,1,0:T(8,128)S(1)} %get-tuple-element.36), channel_id=1, source_target_pairs={{8,16},{16,8},{24,32},{32,24},{40,48},{48,40},{56,0},{64,120},{72,... | collective-permute-start | bytes 1179656 | tf_op jit(solution)/shard_map/ppermute | solution.py:335
  7.5 42.9 %collective-permute-start.2 = (f32[5,2,128,128]{3,2,1,0:T(8,128)}, f32[5,2,128,128]{3,2,1,0:T(8,128)S(1)}, u32[]{:S(2)}, u32[]{:S(2)}) collective-permute-start(f32[5,2,128,128]{3,2,1,0:T(8,128)} %get-tuple-element.35), channel_id=1, source_target_pairs={{8,16},{16,8},{24,32},{32,24},{40,48},{48,40},{56,64},{64,56},{72,... | collective-permute-start | bytes 1966088 | tf_op jit(solution)/shard_map/ppermute | solution.py:334
  9.4 28.8 %collective-permute-start.1 = (f32[1,2,128,128]{3,2,1,0:T(8,128)}, f32[1,2,128,128]{3,2,1,0:T(8,128)S(1)}, u32[]{:S(2)}, u32[]{:S(2)}) collective-permute-start(f32[1,2,128,128]{3,2,1,0:T(8,128)} %own_ref.1), channel_id=1, source_target_pairs={{0,8},{8,16},{16,24},{24,32},{32,40},{40,48},{48,56},{56,64},{64,7... | collective-permute-start | bytes 393224 | tf_op jit(solution)/shard_map/ppermute | solution.py:299
  13.0 37.4 %collective-permute-start.4 = (f32[3,2,128,128]{3,2,1,0:T(8,128)S(1)}, f32[3,2,128,128]{3,2,1,0:T(8,128)S(1)}, u32[]{:S(2)}, u32[]{:S(2)}) collective-permute-start(f32[3,2,128,128]{3,2,1,0:T(8,128)S(1)} %collective-permute-done.3.rb_ref), channel_id=1, source_target_pairs={{0,64},{120,56},{64,128},{184,120},{128,192},{248,184},{1,65},{121... | collective-permute-start | bytes 1179656 | tf_op jit(solution)/shard_map/ppermute | solution.py:339
  16.1 34.2 %collective-permute-start.5 = (f32[2,2,128,128]{3,2,1,0:T(8,128)}, f32[2,2,128,128]{3,2,1,0:T(8,128)S(1)}, u32[]{:S(2)}, u32[]{:S(2)}) collective-permute-start(f32[2,2,128,128]{3,2,1,0:T(8,128)} %get-tuple-element.37), channel_id=1, source_target_pairs={{0,1},{1,0},{2,3},{3,2},{4,5},{5,4},{6,7},{7,6},{8,9},{9,8},{10,11... | collective-permute-start | bytes 786440 | tf_op jit(solution)/shard_map/ppermute | solution.py:337
  38.2 2.7 %copy-start.5 = (s32[128,2]{0,1:T(2,128)S(1)}, s32[128,2]{0,1:T(2,128)}, u32[]{:S(2)}) copy-start(s32[128,2]{0,1:T(2,128)} %param.7) | copy-start | bytes 3076
  38.2 12.2 %collective-permute-start.6 = (f32[2,2,128,128]{3,2,1,0:T(8,128)S(1)}, f32[2,2,128,128]{3,2,1,0:T(8,128)S(1)}, u32[]{:S(2)}, u32[]{:S(2)}) collective-permute-start(f32[2,2,128,128]{3,2,1,0:T(8,128)S(1)} %get-tuple-element.38), channel_id=1, source_target_pairs={{1,2},{2,1},{3,4},{4,3},{5,6},{6,5},{9,10},{10,9},{11,12},{12,11},... | collective-permute-start | bytes 786440 | tf_op jit(solution)/shard_map/ppermute | solution.py:336
  40.9 0.7 copy-start.4
  41.5 1.0 copy-start.2
  42.6 0.9 copy-start.3
  51.9 17.3 %collective-permute-start.7 = (f32[8,2,128,128]{3,2,1,0:T(8,128)S(1)}, f32[8,2,128,128]{3,2,1,0:T(8,128)S(1)}, u32[]{:S(2)}, u32[]{:S(2)}) collective-permute-start(f32[8,2,128,128]{3,2,1,0:T(8,128)S(1)} %get-tuple-element.40.w_ref), channel_id=1, source_target_pairs={{0,8},{8,0},{16,24},{24,16},{32,40},{40,32},{48,56},{56,48},{64,72... | collective-permute-start | bytes 3145736 | tf_op jit(solution)/shard_map/ppermute | solution.py:338
  52.0 10.3 %collective-permute-start.9 = (f32[3,2,128,128]{3,2,1,0:T(8,128)S(1)}, f32[3,2,128,128]{3,2,1,0:T(8,128)S(1)}, u32[]{:S(2)}, u32[]{:S(2)}) collective-permute-start(f32[3,2,128,128]{3,2,1,0:T(8,128)S(1)} %get-tuple-element.42), channel_id=1, source_target_pairs={{8,16},{16,8},{24,32},{32,24},{40,48},{48,40},{56,0},{64,120},{72,... | collective-permute-start | bytes 1179656 | tf_op jit(solution)/shard_map/ppermute | solution.py:335
  53.9 31.7 %collective-permute-start.8 = (f32[5,2,128,128]{3,2,1,0:T(8,128)S(1)}, f32[5,2,128,128]{3,2,1,0:T(8,128)S(1)}, u32[]{:S(2)}, u32[]{:S(2)}) collective-permute-start(f32[5,2,128,128]{3,2,1,0:T(8,128)S(1)} %get-tuple-element.41), channel_id=1, source_target_pairs={{8,16},{16,8},{24,32},{32,24},{40,48},{48,40},{56,64},{64,56},{72,... | collective-permute-start | bytes 1966088 | tf_op jit(solution)/shard_map/ppermute | solution.py:334
  62.3 23.4 %collective-permute-start.10 = (f32[3,2,128,128]{3,2,1,0:T(8,128)S(1)}, f32[3,2,128,128]{3,2,1,0:T(8,128)S(1)}, u32[]{:S(2)}, u32[]{:S(2)}) collective-permute-start(f32[3,2,128,128]{3,2,1,0:T(8,128)S(1)} %collective-permute-done.9.rb_ref), channel_id=1, source_target_pairs={{0,64},{120,56},{64,128},{184,120},{128,192},{248,184},{1,65},{121... | collective-permute-start | bytes 1179656 | tf_op jit(solution)/shard_map/ppermute | solution.py:339
  64.2 15.7 %collective-permute-start.11 = (f32[2,2,128,128]{3,2,1,0:T(8,128)S(1)}, f32[2,2,128,128]{3,2,1,0:T(8,128)S(1)}, u32[]{:S(2)}, u32[]{:S(2)}) collective-permute-start(f32[2,2,128,128]{3,2,1,0:T(8,128)S(1)} %get-tuple-element.43), channel_id=1, source_target_pairs={{0,1},{1,0},{2,3},{3,2},{4,5},{5,4},{6,7},{7,6},{8,9},{9,8},{10,11... | collective-permute-start | bytes 786440 | tf_op jit(solution)/shard_map/ppermute | solution.py:337
  64.3 21.3 %collective-permute-start.12 = (f32[2,2,128,128]{3,2,1,0:T(8,128)S(1)}, f32[2,2,128,128]{3,2,1,0:T(8,128)S(1)}, u32[]{:S(2)}, u32[]{:S(2)}) collective-permute-start(f32[2,2,128,128]{3,2,1,0:T(8,128)S(1)} %get-tuple-element.44), channel_id=1, source_target_pairs={{1,2},{2,1},{3,4},{4,3},{5,6},{6,5},{9,10},{10,9},{11,12},{12,11},... | collective-permute-start | bytes 786440 | tf_op jit(solution)/shard_map/ppermute | solution.py:336
  87.2 16.5 %collective-permute-start.13 = (f32[8,2,128,128]{3,2,1,0:T(8,128)S(1)}, f32[8,2,128,128]{3,2,1,0:T(8,128)S(1)}, u32[]{:S(2)}, u32[]{:S(2)}) collective-permute-start(f32[8,2,128,128]{3,2,1,0:T(8,128)S(1)} %get-tuple-element.45.w_ref), channel_id=1, source_target_pairs={{0,8},{8,0},{16,24},{24,16},{32,40},{40,32},{48,56},{56,48},{64,72... | collective-permute-start | bytes 3145736 | tf_op jit(solution)/shard_map/ppermute | solution.py:338
  87.3 10.3 %collective-permute-start.15 = (f32[3,2,128,128]{3,2,1,0:T(8,128)S(1)}, f32[3,2,128,128]{3,2,1,0:T(8,128)S(1)}, u32[]{:S(2)}, u32[]{:S(2)}) collective-permute-start(f32[3,2,128,128]{3,2,1,0:T(8,128)S(1)} %get-tuple-element.47), channel_id=1, source_target_pairs={{8,16},{16,8},{24,32},{32,24},{40,48},{48,40},{56,0},{64,120},{72,... | collective-permute-start | bytes 1179656 | tf_op jit(solution)/shard_map/ppermute | solution.py:335
  89.2 31.8 %collective-permute-start.14 = (f32[5,2,128,128]{3,2,1,0:T(8,128)S(1)}, f32[5,2,128,128]{3,2,1,0:T(8,128)S(1)}, u32[]{:S(2)}, u32[]{:S(2)}) collective-permute-start(f32[5,2,128,128]{3,2,1,0:T(8,128)S(1)} %get-tuple-element.46), channel_id=1, source_target_pairs={{8,16},{16,8},{24,32},{32,24},{40,48},{48,40},{56,64},{64,56},{72,... | collective-permute-start | bytes 1966088 | tf_op jit(solution)/shard_map/ppermute | solution.py:334
  97.6 23.4 %collective-permute-start.16 = (f32[3,2,128,128]{3,2,1,0:T(8,128)S(1)}, f32[3,2,128,128]{3,2,1,0:T(8,128)S(1)}, u32[]{:S(2)}, u32[]{:S(2)}) collective-permute-start(f32[3,2,128,128]{3,2,1,0:T(8,128)S(1)} %collective-permute-done.15.rb_ref), channel_id=1, source_target_pairs={{0,64},{120,56},{64,128},{184,120},{128,192},{248,184},{1,65},{121... | collective-permute-start | bytes 1179656 | tf_op jit(solution)/shard_map/ppermute | solution.py:339
  99.5 15.7 %collective-permute-start.17 = (f32[2,2,128,128]{3,2,1,0:T(8,128)S(1)}, f32[2,2,128,128]{3,2,1,0:T(8,128)S(1)}, u32[]{:S(2)}, u32[]{:S(2)}) collective-permute-start(f32[2,2,128,128]{3,2,1,0:T(8,128)S(1)} %get-tuple-element.48), channel_id=1, source_target_pairs={{0,1},{1,0},{2,3},{3,2},{4,5},{5,4},{6,7},{7,6},{8,9},{9,8},{10,11... | collective-permute-start | bytes 786440 | tf_op jit(solution)/shard_map/ppermute | solution.py:337
  99.6 21.4 %collective-permute-start.18 = (f32[2,2,128,128]{3,2,1,0:T(8,128)S(1)}, f32[2,2,128,128]{3,2,1,0:T(8,128)S(1)}, u32[]{:S(2)}, u32[]{:S(2)}) collective-permute-start(f32[2,2,128,128]{3,2,1,0:T(8,128)S(1)} %get-tuple-element.49), channel_id=1, source_target_pairs={{1,2},{2,1},{3,4},{4,3},{5,6},{6,5},{9,10},{10,9},{11,12},{12,11},... | collective-permute-start | bytes 786440 | tf_op jit(solution)/shard_map/ppermute | solution.py:336
  122.4 17.9 %collective-permute-start.19 = (f32[8,2,128,128]{3,2,1,0:T(8,128)S(1)}, f32[8,2,128,128]{3,2,1,0:T(8,128)S(1)}, u32[]{:S(2)}, u32[]{:S(2)}) collective-permute-start(f32[8,2,128,128]{3,2,1,0:T(8,128)S(1)} %get-tuple-element.50.w_ref), channel_id=1, source_target_pairs={{0,8},{8,0},{16,24},{24,16},{32,40},{40,32},{48,56},{56,48},{64,72... | collective-permute-start | bytes 3145736 | tf_op jit(solution)/shard_map/ppermute | solution.py:338
  122.5 10.3 %collective-permute-start.21 = (f32[3,2,128,128]{3,2,1,0:T(8,128)S(1)}, f32[3,2,128,128]{3,2,1,0:T(8,128)S(1)}, u32[]{:S(2)}, u32[]{:S(2)}) collective-permute-start(f32[3,2,128,128]{3,2,1,0:T(8,128)S(1)} %get-tuple-element.52), channel_id=1, source_target_pairs={{8,16},{16,8},{24,32},{32,24},{40,48},{48,40},{56,0},{64,120},{72,... | collective-permute-start | bytes 1179656 | tf_op jit(solution)/shard_map/ppermute | solution.py:335
  124.5 31.8 %collective-permute-start.20 = (f32[5,2,128,128]{3,2,1,0:T(8,128)S(1)}, f32[5,2,128,128]{3,2,1,0:T(8,128)S(1)}, u32[]{:S(2)}, u32[]{:S(2)}) collective-permute-start(f32[5,2,128,128]{3,2,1,0:T(8,128)S(1)} %get-tuple-element.51), channel_id=1, source_target_pairs={{8,16},{16,8},{24,32},{32,24},{40,48},{48,40},{56,64},{64,56},{72,... | collective-permute-start | bytes 1966088 | tf_op jit(solution)/shard_map/ppermute | solution.py:334
  132.9 23.4 %collective-permute-start.22 = (f32[3,2,128,128]{3,2,1,0:T(8,128)S(1)}, f32[3,2,128,128]{3,2,1,0:T(8,128)S(1)}, u32[]{:S(2)}, u32[]{:S(2)}) collective-permute-start(f32[3,2,128,128]{3,2,1,0:T(8,128)S(1)} %collective-permute-done.21.rb_ref), channel_id=1, source_target_pairs={{0,64},{120,56},{64,128},{184,120},{128,192},{248,184},{1,65},{121... | collective-permute-start | bytes 1179656 | tf_op jit(solution)/shard_map/ppermute | solution.py:339
  134.8 15.7 %collective-permute-start.23 = (f32[2,2,128,128]{3,2,1,0:T(8,128)S(1)}, f32[2,2,128,128]{3,2,1,0:T(8,128)S(1)}, u32[]{:S(2)}, u32[]{:S(2)}) collective-permute-start(f32[2,2,128,128]{3,2,1,0:T(8,128)S(1)} %get-tuple-element.53), channel_id=1, source_target_pairs={{0,1},{1,0},{2,3},{3,2},{4,5},{5,4},{6,7},{7,6},{8,9},{9,8},{10,11... | collective-permute-start | bytes 786440 | tf_op jit(solution)/shard_map/ppermute | solution.py:337
  134.9 21.4 %collective-permute-start.24 = (f32[2,2,128,128]{3,2,1,0:T(8,128)S(1)}, f32[2,2,128,128]{3,2,1,0:T(8,128)S(1)}, u32[]{:S(2)}, u32[]{:S(2)}) collective-permute-start(f32[2,2,128,128]{3,2,1,0:T(8,128)S(1)} %get-tuple-element.54), channel_id=1, source_target_pairs={{1,2},{2,1},{3,4},{4,3},{5,6},{6,5},{9,10},{10,9},{11,12},{12,11},... | collective-permute-start | bytes 786440 | tf_op jit(solution)/shard_map/ppermute | solution.py:336
